TPU v7x, 32 devices: a whole 2x2x4 slice. The times are simulated.
32 devices in a mesh: seq: 8 (over z, y), head: 4 (over x, core).
Axes of the slice: x: 2, y: 2, z: 4, core: 2. Of those that a mesh axis runs over, the one named last changes fastest.
Arguments:
- query: bfloat16 [8192, 4096], P('seq', 'head'), may hold values from -0.15625 to 0.15625
- key: bfloat16 [8192, 4096], P('seq', 'head'), may hold values from -0.15625 to 0.15625
- value: bfloat16 [8192, 4096], P('seq', 'head'), may hold values from -18 to 18, as said below
- level_coef: float32 [4, 32, 8192], P(None, 'head', 'seq'), may hold values from 0.25 to 2.5
- gain: float32 [4096], P('head'), may hold values from 0.5 to 1.5
- cotangent: bfloat16 [8192, 4096], P('seq', 'head'), may hold values from -0.625 to 0.625
Outputs:
- mixed: bfloat16 [8192, 4096], P('seq', 'head')
- grad_query: bfloat16 [8192, 4096], P('seq', 'head')
- grad_key: bfloat16 [8192, 4096], P('seq', 'head')
- grad_value: bfloat16 [8192, 4096], P('seq', 'head')
- grad_level: float32 [4, 32, 8192], P(None, 'head', 'seq')
- grad_gain: float32 [4096], P('head')
Inputs may be any that keep to these rules, and one draw needn't show every extreme that they name: `value`: real values.
All inputs are finite; a program needn't handle non-finite values.
Results may differ from a plain program's by a relative error of at most 0.0065.
Values sent between devices are 32-bit elements; how exact they have to be, the bound alone decides.
No kernel may reach another device: no remote copies, remote signals or barrier semaphores. Data moves between devices by JAX's collectives and lax.ppermute only.
A program may use at most 128 MiB of HBM per device.

v0:
```python
import jax
import jax.numpy as jnp
from jax import lax
from jax.sharding import PartitionSpec as P

HEADS = 32
HEAD_DIM = 128


EPS = 1e-06


def from_partner(block, axis, apart):
    count = lax.axis_size(axis)
    route = []
    for low in range(count):
        high = low | 1 << apart
        if high != low and high < count:
            route += [(low, high), (high, low)]
    return lax.ppermute(block, axis, route)


def body(query, key, value, level_coef, gain, cotangent):
    f32 = jnp.float32
    bf16 = jnp.bfloat16
    rows = query.shape[0]
    heads_here = level_coef.shape[1]
    width = query.shape[1] // heads_here
    depth = level_coef.shape[0] - 1
    group = lax.axis_index("seq")
    q_three = query.reshape(rows, heads_here, width)
    k_three = key.reshape(rows, heads_here, width)
    v_three = value.reshape(rows, heads_here, width)
    scores = jnp.einsum("the,she->hts", q_three, k_three, preferred_element_type=f32)
    causal = lax.broadcasted_iota(jnp.int32, (rows, rows), 0) >= lax.broadcasted_iota(
        jnp.int32, (rows, rows), 1
    )
    kept = jnp.where(causal[None], scores, 0.0).astype(bf16)
    local = jnp.einsum("hts,she->the", kept, v_three, preferred_element_type=f32)
    states = jnp.einsum("sha,shb->hab", k_three, v_three, preferred_element_type=f32)
    bits = [(group // 2**level % 2).astype(f32) for level in range(depth)]
    block = states
    found = []
    for level in range(depth):
        other = from_partner(block, "seq", level)
        found.append(bits[level] * other)
        block = block + other
    buckets = jnp.stack(found)
    bucket_half = buckets.astype(bf16)
    reads = jnp.einsum("the,lhef->lthf", q_three, bucket_half, preferred_element_type=f32)
    first = level_coef[0].T[:, :, None]
    rest = level_coef[1:].transpose(0, 2, 1)[..., None]
    output = first * local + jnp.sum(rest * reads, axis=0)
    squares = lax.psum(jnp.sum(output * output, axis=(1, 2)), "head")
    scale = lax.rsqrt(squares / (HEADS * HEAD_DIM) + EPS)[:, None, None]
    normed = output * scale
    gain_three = gain.reshape(heads_here, width)
    mixed = (normed * gain_three).astype(bf16).reshape(rows, -1)
    cot_three = cotangent.reshape(rows, heads_here, width).astype(f32)
    grad_gain = lax.psum(jnp.sum(cot_three * normed, axis=0).reshape(-1), "seq")
    weighted_cot = cot_three * gain_three
    inner = lax.psum(jnp.sum(weighted_cot * output, axis=(1, 2)), "head")
    grad_full = (
        weighted_cot - output * (inner[:, None, None] * scale * scale / (HEADS * HEAD_DIM))
    ) * scale
    grad_half = grad_full.astype(bf16)
    grad_float = grad_half.astype(f32)
    grad_first = jnp.sum(grad_float * local, axis=-1)
    grad_rest = jnp.sum(grad_float[None] * reads, axis=-1)
    grad_level = jnp.concatenate([grad_first.T[None], grad_rest.transpose(0, 2, 1)], axis=0)
    weighted = (first * grad_float).astype(bf16)
    value_sum = jnp.einsum("hts,the->she", kept, weighted, preferred_element_type=f32)
    pair = (
        jnp.einsum("the,she->hts", grad_half, v_three, preferred_element_type=f32)
        * level_coef[0][:, :, None]
    )
    pair = jnp.where(causal[None], pair, 0.0).astype(bf16)
    query_sum = jnp.einsum("hts,she->the", pair, k_three, preferred_element_type=f32)
    key_sum = jnp.einsum("hts,the->she", pair, q_three, preferred_element_type=f32)
    scaled = (rest * grad_float[None]).astype(bf16)
    query_sum = query_sum + jnp.einsum(
        "lthf,lhef->the", scaled, bucket_half, preferred_element_type=f32
    )
    grad_buckets = jnp.einsum("the,lthf->lhef", q_three, scaled, preferred_element_type=f32)
    masks = jnp.stack(bits)[:, None, None, None]
    pending = masks * grad_buckets
    carried = jnp.zeros_like(states)
    for level in range(depth):
        other = from_partner(pending, "seq", level)
        carried = carried + (1.0 - bits[level]) * other[0]
        pending = pending[1:] + other[1:]
    grad_states = carried.astype(bf16)
    key_sum = key_sum + jnp.einsum("shb,hab->sha", v_three, grad_states, preferred_element_type=f32)
    value_sum = value_sum + jnp.einsum(
        "sha,hab->shb", k_three, grad_states, preferred_element_type=f32
    )
    grad_query = query_sum.astype(bf16).reshape(rows, -1)
    grad_key = key_sum.astype(bf16).reshape(rows, -1)
    grad_value = value_sum.astype(bf16).reshape(rows, -1)
    return (mixed, grad_query, grad_key, grad_value, grad_level, grad_gain)


def solution(mesh):
    placed = (
        P("seq", "head"),
        P("seq", "head"),
        P("seq", "head"),
        P(None, "head", "seq"),
        P("head"),
        P("seq", "head"),
    )
    return jax.shard_map(
        body,
        mesh=mesh,
        in_specs=placed,
        out_specs=(
            P("seq", "head"),
            P("seq", "head"),
            P("seq", "head"),
            P("seq", "head"),
            P(None, "head", "seq"),
            P("head"),
        ),
        check_vma=False,
    )
```

profile of v0, /device:TPU:0, one launch (start us, length us, event | category | flops | bytes accessed | tf_op | source)
XLA Modules:
  0.0 245.2 jit_solution(4690820925191589461)
XLA Ops:
  0.6 3.7 %copy.75 = bf16[128,8,8,128]{3,2,1,0:T(8,128)(2,1)} copy(bf16[128,8,8,128]{3,1,2,0:T(8,128)(2,1)} %bitcast.130) | data formatting | bytes 4194304
  4.3 4.1 %copy.39 = bf16[1024,8,128]{0,2,1:T(8,128)(2,1)} copy(bf16[1024,8,128]{2,1,0:T(8,128)(2,1)} %bitcast.129) | data formatting | bytes 4194304 | tf_op jit(solution)/shard_map/reshape | solution.py:32
  10.8 3.1 %collective-permute-start = (f32[8,128,128]{2,1,0:T(8,128)S(1)}, f32[8,128,128]{2,1,0:T(8,128)}, u32[]{:S(2)}, u32[]{:S(2)}) collective-permute-start(f32[8,128,128]{2,1,0:T(8,128)S(1)} %fusion.15), channel_id=1, source_target_pairs={{0,4},{4,0},{8,12},{12,8},{16,20},{20,16},{24,28},{28,24},{1,5},{5... | collective-permute-start | bytes 1572872 | tf_op jit(solution)/shard_map/ppermute | solution.py:20
  13.9 3.5 %copy.74 = bf16[128,8,8,128]{3,2,1,0:T(8,128)(2,1)} copy(bf16[128,8,8,128]{3,1,2,0:T(8,128)(2,1)} %bitcast.133) | data formatting | bytes 4194304
  17.4 4.1 %copy.49 = bf16[1024,8,128]{0,2,1:T(8,128)(2,1)} copy(bf16[1024,8,128]{2,1,0:T(8,128)(2,1)} %bitcast.122) | data formatting | bytes 4194304 | tf_op jit(solution)/shard_map/reshape | solution.py:31
  21.8 4.1 %collective-permute-done = f32[8,128,128]{2,1,0:T(8,128)} collective-permute-done((f32[8,128,128]{2,1,0:T(8,128)S(1)}, f32[8,128,128]{2,1,0:T(8,128)}, u32[]{:S(2)}, u32[]{:S(2)}) %collective-permute-start) | collective-permute-done | bytes 524320 | tf_op jit(solution)/shard_map/ppermute | solution.py:20
  29.1 10.4 %select_convert_fusion.1 = bf16[8,1024,1024]{2,1,0:T(8,128)(2,1)} fusion(pred[1024,1024]{1,0:T(8,128)(4,1)S(1)} %iota_compare_fusion, bf16[1024,8,128]{0,2,1:T(8,128)(2,1)} %copy.49, bf16[1024,1024]{1,0:T(8,128)(2,1)} %param.7), kind=kOutput, calls=%fused_computation.1 | convolution fusion | flops 2164260864 | bytes 22020096 | tf_op jit(solution)/shard_map/the,she->hts/dot_general | solution.py:34
  45.0 4.1 %copy.43 = f32[1024,1024]{0,1:T(8,128)} copy(bf16[1024,1024]{1,0:T(8,128)(2,1)} %param.11) | data formatting | bytes 6291456 | tf_op jit(solution)/shard_map/convert_element_type | solution.py:59
  49.2 17.9 %collective-permute-done.2 = f32[8,128,128]{2,1,0:T(8,128)} collective-permute-done((f32[8,128,128]{2,1,0:T(8,128)}, f32[8,128,128]{2,1,0:T(8,128)}, u32[]{:S(2)}, u32[]{:S(2)}) %collective-permute-start.2) | collective-permute-done | bytes 524320 | tf_op jit(solution)/shard_map/ppermute | solution.py:20
  68.1 10.4 %fusion = (f32[1024,8,128]{0,2,1:T(8,128)}, f32[8,3,128,1024]{3,2,1,0:T(8,128)}) fusion(f32[3,1024,8]{1,0,2:T(4,128)S(1)} %copy.38, bf16[1024,8,128,1]{2,1,0,3:T(8,128)(2,1)} %bitcast.123, bf16[1,8,128,128]{3,2,1,0:T(8,128)(2,1)S(1)} %fusion.39, bf16[1,8,128,128]{3,2,1,0:T(8,128)(2,1)S(1)} %get-tuple-element.29, ...), kind=kOutput, calls=%fused_computation.4 | convolution fusion | flops 811335680 | bytes 19759104 | tf_op jit(solution)/shard_map/the,lhef->lthf/dot_general | solution.py:50
  78.5 12.1 %multiply_reduce_fusion.2 = (f32[1024]{0:T(1024)S(1)}, f32[1024,8,128]{0,2,1:T(8,128)}, f32[8,1024,128]{1,2,0:T(8,128)}) fusion(f32[1024,8,128]{0,2,1:T(8,128)} %get-tuple-element.33, f32[1024,8]{0,1:T(8,128)S(1)} %get-tuple-element.32, bf16[8,1024,1024]{2,1,0:T(8,128)(2,1)} %select_convert_fusion.1, bf16[1024,1024]{1,0:T(8,128)(2,1)S(1)} %copy-done), kind=kOutput, calls=%fused_computation.23 | convolution fusion | flops 2151676928 | bytes 31494144 | tf_op jit(solution)/shard_map/hts,she->the/dot_general | solution.py:39
  90.6 5.6 %psum.21 = f32[1024]{0:T(1024)S(1)} all-reduce(f32[1024]{0:T(1024)S(1)} %get-tuple-element.22), channel_id=1, replica_groups=mesh['seq'=8,'head'=4] {'head'}, use_global_device_ids=true, to_apply=%region_2.3 | all-reduce | flops 1024 | bytes 8192 | tf_op jit(solution)/shard_map/psum | solution.py:54
  96.2 5.7 %multiply_reduce_fusion = (f32[8,128]{1,0:T(8,128)S(1)}, f32[1024]{0:T(1024)S(1)}) fusion(f32[1024,8,128]{0,2,1:T(8,128)} %bitcast.121, f32[1024,8,128]{0,2,1:T(8,128)} %get-tuple-element.23, f32[1024]{0:T(1024)S(1)} %add_rsqrt_fusion, f32[8,128]{1,0:T(8,128)S(1)} %bitcast.136, f32[1024,1024]{0,1:T(8,128)} %copy.43), kind=kLoop, calls=%fused_computation.17 | loop fusion | flops 6289408 | bytes 12599296 | tf_op jit(solution)/shard_map/reduce_sum | solution.py:60
  101.9 6.5 %psum.22 = f32[1024]{0:T(1024)S(1)} all-reduce(f32[1024]{0:T(1024)S(1)} %get-tuple-element.19), channel_id=1, replica_groups=mesh['seq'=8,'head'=4] {'head'}, use_global_device_ids=true, to_apply=%region_4.5 | all-reduce | flops 1024 | bytes 8192 | tf_op jit(solution)/shard_map/psum | solution.py:62
  108.5 6.7 %fusion.7 = (f32[1024,8]{0,1:T(8,128)S(1)}, bf16[1024,8,128]{0,2,1:T(8,128)(2,1)S(1)}, bf16[1024,8,128]{0,2,1:T(8,128)(2,1)}) fusion(f32[8,1024,128]{1,2,0:T(8,128)} %get-tuple-element.35, f32[1024]{0:T(1024)S(1)} %add_rsqrt_fusion, f32[1024,8,128]{0,2,1:T(8,128)} %get-tuple-element.23, f32[1024]{0:T(1024)S(1)} %fusion.41, f32[8,128]{1,0:T(8,128)S(1)} %bitcast.137, ...), kind=kLoop, calls=%fused_computation.16 | loop fusion | flops 11526144 | bytes 16822272 | tf_op jit(solution)/shard_map/reduce_sum | solution.py:68
  118.3 4.3 %fusion.1 = (f32[3,1024,8]{1,0,2:T(4,128)S(1)}, bf16[3,1024,8,128]{1,3,0,2:T(8,128)(2,1)}) fusion(f32[8,3,128,1024]{3,2,1,0:T(8,128)S(1)} %bitcast.118, f32[1024,8,128]{0,2,1:T(8,128)S(1)} %convert_element_type.64, f32[3,1024,8]{1,0,2:T(4,128)S(1)} %copy.38), kind=kLoop, calls=%fused_computation.5 | loop fusion | flops 12558336 | bytes 23265280 | tf_op jit(solution)/shard_map/reduce_sum | solution.py:69
  123.4 3.0 %multiply_bitcast_fusion = f32[3,8,128,128]{2,3,0,1:T(8,128)} fusion(bf16[1024,8,128,1]{2,1,0,3:T(8,128)(2,1)S(1)} %bitcast.124, f32[3]{0:T(128)S(1)} %pad_maximum_fusion.2, f32[1024,8,128]{0,2,1:T(8,128)S(1)} %convert_element_type.64, f32[3,1024,8]{1,0,2:T(4,128)S(1)} %copy.38), kind=kOutput, calls=%fused_computation.42 | convolution fusion | flops 811991040 | bytes 7962636 | tf_op jit(solution)/shard_map/the,lthf->lhef/dot_general | solution.py:84
  127.6 9.6 %select_convert_fusion = bf16[8,1024,1024]{2,1,0:T(8,128)(2,1)} fusion(f32[8,1024]{1,0:T(8,128)S(1)} %get-tuple-element.31, pred[1024,1024]{1,0:T(8,128)(4,1)S(1)} %copy-done.4, bf16[1024,8,128]{0,2,1:T(8,128)(2,1)S(1)} %get-tuple-element.21, bf16[1024,1024]{1,0:T(8,128)(2,1)S(1)} %copy-done), kind=kOutput, calls=%fused_computation | convolution fusion | flops 2172649472 | bytes 22052864 | tf_op jit(solution)/shard_map/the,she->hts/dot_general | solution.py:74
  137.3 11.4 %fusion.43 = f32[8,1024,128]{1,2,0:T(8,128)} fusion(bf16[8,1024,1024]{2,1,0:T(8,128)(2,1)} %select_convert_fusion, bf16[1024,8,128]{0,2,1:T(8,128)(2,1)} %copy.39), kind=kOutput, calls=%fused_computation.71 | convolution fusion | flops 2147483648 | bytes 23068672 | tf_op jit(solution)/shard_map/hts,she->the/dot_general | solution.py:78
  148.7 10.9 %fusion.10 = f32[8,128,1024]{2,1,0:T(8,128)} fusion(bf16[8,1024,1024]{2,1,0:T(8,128)(2,1)} %select_convert_fusion.1, bf16[1024,8,128]{0,2,1:T(8,128)(2,1)} %copy-done.2, f32[1024,8]{0,1:T(8,128)S(1)} %get-tuple-element.32), kind=kOutput, calls=%fused_computation.25 | convolution fusion | flops 2150629376 | bytes 23101440 | tf_op jit(solution)/shard_map/hts,the->she/dot_general | solution.py:72
  162.0 2.8 %slice_add_fusion = f32[2,8,128,128]{2,3,0,1:T(8,128)} fusion(f32[3,8,128,128]{2,3,0,1:T(8,128)} %collective-permute-done.3, f32[3,8,128,128]{2,3,0,1:T(8,128)} %multiply_bitcast_fusion), kind=kLoop, calls=%fused_computation.47 | loop fusion | flops 262144 | bytes 3145728 | tf_op jit(solution)/shard_map/add | solution.py:91
  166.3 6.1 %fusion.44 = f32[8,1024,128]{1,2,0:T(8,128)} fusion(bf16[1024,8,128]{0,2,1:T(8,128)(2,1)} %copy.49, bf16[8,1024,1024]{2,1,0:T(8,128)(2,1)S(1)} %bitcast.120), kind=kOutput, calls=%fused_computation.72 | convolution fusion | flops 2147483648 | bytes 23068672 | tf_op jit(solution)/shard_map/hts,the->she/dot_general | solution.py:79
  172.4 16.3 %collective-permute-done.4 = f32[2,8,128,128]{2,3,0,1:T(8,128)} collective-permute-done((f32[2,8,128,128]{2,3,0,1:T(8,128)}, f32[2,8,128,128]{2,3,0,1:T(8,128)}, u32[]{:S(2)}, u32[]{:S(2)}) %collective-permute-start.4) | collective-permute-done | bytes 1048608 | tf_op jit(solution)/shard_map/ppermute | solution.py:20
  190.0 3.4 %collective-permute-start.5 = (f32[1,8,128,128]{2,3,0,1:T(8,128)S(1)}, f32[1,8,128,128]{2,3,0,1:T(8,128)}, u32[]{:S(2)}, u32[]{:S(2)}) collective-permute-start(f32[1,8,128,128]{2,3,0,1:T(8,128)S(1)} %slice_add_fusion.1), channel_id=1, source_target_pairs={{0,16},{16,0},{4,20},{20,4},{8,24},{24,8},{12,28},{28,12},{1,17},{... | collective-permute-start | bytes 1572872 | tf_op jit(solution)/shard_map/ppermute | solution.py:20
  193.4 4.8 %fusion.4 = bf16[1024,8,128]{0,2,1:T(8,128)(2,1)} fusion(f32[8,1024,128]{1,2,0:T(8,128)} %fusion.43, bf16[3,1024,8,128]{1,3,0,2:T(8,128)(2,1)S(1)} %bitcast.126, bf16[1,8,128,128]{3,2,1,0:T(8,128)(2,1)S(1)} %fusion.39, bf16[1,8,128,128]{3,2,1,0:T(8,128)(2,1)S(1)} %get-tuple-element.29, bf16[1,8,128,128]{3,2,1,0:T(8,128)(2,1)S(1)} %get-tuple-element.27), kind=kOutput, calls=%fused_computation.10 | convolution fusion | flops 808189952 | bytes 13369344 | tf_op jit(solution)/shard_map/lthf,lhef->the/dot_general | solution.py:81
  198.2 3.9 %copy.55 = bf16[1024,1024]{1,0:T(8,128)(2,1)} copy(bf16[1024,1024]{0,1:T(8,128)(2,1)} %bitcast.128) | data formatting | bytes 4194304
  202.1 3.9 %copy.54 = bf16[1024,1024]{1,0:T(8,128)(2,1)} copy(bf16[1024,1024]{0,1:T(8,128)(2,1)} %bitcast.127) | data formatting | bytes 4194304
  206.0 20.6 %psum.23 = f32[1024]{0:T(1024)} all-reduce(f32[1024]{0:T(1024)S(1)} %bitcast.138), channel_id=1, replica_groups=mesh['seq'=8,'head'=4] {'seq'}, use_global_device_ids=true, to_apply=%region_8.9 | all-reduce | flops 1024 | bytes 8192 | tf_op jit(solution)/shard_map/psum | solution.py:60
  228.1 4.9 %add_convert_fusion = bf16[8,128,1024]{2,1,0:T(8,128)(2,1)} fusion(f32[8,128,1024]{2,1,0:T(8,128)} %fusion.10, bf16[8,128,128]{1,2,0:T(8,128)(2,1)S(1)} %fusion.40, bf16[1024,1024]{1,0:T(8,128)(2,1)} %param.7), kind=kOutput, calls=%fused_computation.18 | convolution fusion | flops 270532608 | bytes 8650752 | tf_op jit(solution)/shard_map/sha,hab->shb/dot_general | solution.py:94
  233.0 3.9 %copy.57 = bf16[1024,1024]{1,0:T(8,128)(2,1)} copy(bf16[1024,1024]{0,1:T(8,128)(2,1)} %bitcast.132) | data formatting | bytes 4194304
  236.9 4.3 %fusion.5 = bf16[1024,8,128]{0,2,1:T(8,128)(2,1)} fusion(f32[8,1024,128]{1,2,0:T(8,128)} %fusion.44, bf16[8,128,128]{1,2,0:T(8,128)(2,1)S(1)} %fusion.40, bf16[1024,1024]{1,0:T(8,128)(2,1)S(1)} %copy-done), kind=kOutput, calls=%fused_computation.12 | convolution fusion | flops 270532608 | bytes 8650752 | tf_op jit(solution)/shard_map/shb,hab->sha/dot_general | solution.py:93
  241.3 3.9 %copy.56 = bf16[1024,1024]{1,0:T(8,128)(2,1)} copy(bf16[1024,1024]{0,1:T(8,128)(2,1)} %bitcast.131) | data formatting | bytes 4194304
  (61 shorter events, 24.4 us)
Async XLA Ops:
  0.6 7.8 %copy-start = (bf16[1024,1024]{1,0:T(8,128)(2,1)S(1)}, bf16[1024,1024]{1,0:T(8,128)(2,1)}, u32[]{:S(2)}) copy-start(bf16[1024,1024]{1,0:T(8,128)(2,1)} %param.8) | copy-start | bytes 6291460
  10.8 10.7 %copy-start.5 = (f32[8,128,128]{2,1,0:T(8,128)}, f32[8,128,128]{2,1,0:T(8,128)S(1)}, u32[]{:S(2)}) copy-start(f32[8,128,128]{2,1,0:T(8,128)S(1)} %fusion.15) | copy-start | bytes 1572868
  10.8 15.1 %collective-permute-start = (f32[8,128,128]{2,1,0:T(8,128)S(1)}, f32[8,128,128]{2,1,0:T(8,128)}, u32[]{:S(2)}, u32[]{:S(2)}) collective-permute-start(f32[8,128,128]{2,1,0:T(8,128)S(1)} %fusion.15), channel_id=1, source_target_pairs={{0,4},{4,0},{8,12},{12,8},{16,20},{20,16},{24,28},{28,24},{1,5},{5... | collective-permute-start | bytes 1572872 | tf_op jit(solution)/shard_map/ppermute | solution.py:20
  21.8 7.2 %copy-start.3 = (pred[1024,1024]{1,0:T(8,128)(4,1)}, pred[1024,1024]{1,0:T(8,128)(4,1)S(1)}, u32[]{:S(2)}) copy-start(pred[1024,1024]{1,0:T(8,128)(4,1)S(1)} %iota_compare_fusion) | copy-start | bytes 3145732
  27.2 17.7 %copy-start.6 = (f32[4,8,1024]{2,1,0:T(8,128)S(1)}, f32[4,8,1024]{2,1,0:T(8,128)}, u32[]{:S(2)}) copy-start(f32[4,8,1024]{2,1,0:T(8,128)} %param.9) | copy-start | bytes 393220
  27.2 13.3 %collective-permute-start.1 = (f32[8,128,128]{2,1,0:T(8,128)S(1)}, f32[8,128,128]{2,1,0:T(8,128)}, u32[]{:S(2)}, u32[]{:S(2)}) collective-permute-start(f32[8,128,128]{2,1,0:T(8,128)S(1)} %get-tuple-element.28), channel_id=1, source_target_pairs={{0,8},{8,0},{4,12},{12,4},{16,24},{24,16},{20,28},{28,20},{1,9},{9... | collective-permute-start | bytes 1572872 | tf_op jit(solution)/shard_map/ppermute | solution.py:20
  42.4 24.7 %collective-permute-start.2 = (f32[8,128,128]{2,1,0:T(8,128)}, f32[8,128,128]{2,1,0:T(8,128)}, u32[]{:S(2)}, u32[]{:S(2)}) collective-permute-start(f32[8,128,128]{2,1,0:T(8,128)} %get-tuple-element.30), channel_id=1, source_target_pairs={{0,16},{16,0},{4,20},{20,4},{8,24},{24,8},{12,28},{28,12},{1,17},{... | collective-permute-start | bytes 1572872 | tf_op jit(solution)/shard_map/ppermute | solution.py:20
  78.5 17.7 %copy-start.7 = (f32[1024]{0:T(1024)S(1)}, f32[1024]{0:T(1024)}, u32[]{:S(2)}) copy-start(f32[1024]{0:T(1024)} %param.10) | copy-start | bytes 12292
  108.5 7.2 %slice-start = ((s8[12582912]{0:T(1024)(128)(4,1)}), s8[4194304]{0:T(1024)(128)(4,1)S(1)}, s32[]{:S(2)}) async-start(s8[12582912]{0:T(1024)(128)(4,1)} %bitcast.117), calls=%async_computation | async-start | bytes 8388608
  108.5 8.2 %slice-start.1 = ((s8[12582912]{0:T(1024)(128)(4,1)}), s8[4194304]{0:T(1024)(128)(4,1)S(1)}, s32[]{:S(2)}) async-start(s8[12582912]{0:T(1024)(128)(4,1)} %bitcast.117), calls=%async_computation.1 | async-start | bytes 8388608
  108.5 9.8 %slice-start.2 = ((s8[12582912]{0:T(1024)(128)(4,1)}), s8[4194304]{0:T(1024)(128)(4,1)S(1)}, s32[]{:S(2)}) async-start(s8[12582912]{0:T(1024)(128)(4,1)} %bitcast.117), calls=%async_computation.2 | async-start | bytes 8388608
  115.2 12.4 %copy-start.2 = (bf16[1024,8,128]{0,2,1:T(8,128)(2,1)}, bf16[1024,8,128]{0,2,1:T(8,128)(2,1)S(1)}, u32[]{:S(2)}) copy-start(bf16[1024,8,128]{0,2,1:T(8,128)(2,1)S(1)} %get-tuple-element.21) | copy-start | bytes 6291460
  118.3 5.1 %copy-start.1 = (bf16[128,8,8,128]{3,2,1,0:T(8,128)(2,1)S(1)}, bf16[128,8,8,128]{3,2,1,0:T(8,128)(2,1)}, u32[]{:S(2)}) copy-start(bf16[128,8,8,128]{3,2,1,0:T(8,128)(2,1)} %copy.74) | copy-start | bytes 6291460
  123.4 4.2 %copy-start.4 = (pred[1024,1024]{1,0:T(8,128)(4,1)S(1)}, pred[1024,1024]{1,0:T(8,128)(4,1)}, u32[]{:S(2)}) copy-start(pred[1024,1024]{1,0:T(8,128)(4,1)} %copy-done.3) | copy-start | bytes 3145732
  126.4 35.6 %collective-permute-start.3 = (f32[3,8,128,128]{2,3,0,1:T(8,128)}, f32[3,8,128,128]{2,3,0,1:T(8,128)}, u32[]{:S(2)}, u32[]{:S(2)}) collective-permute-start(f32[3,8,128,128]{2,3,0,1:T(8,128)} %multiply_bitcast_fusion), channel_id=1, source_target_pairs={{0,4},{4,0},{8,12},{12,8},{16,20},{20,16},{24,28},{28,24},{1,5},{5... | collective-permute-start | bytes 4718600 | tf_op jit(solution)/shard_map/ppermute | solution.py:20
  137.3 29.0 %slice-start.3 = ((s8[16777216]{0:T(1024)(128)(4,1)}), s8[4194304]{0:T(1024)(128)(4,1)S(1)}, s32[]{:S(2)}) async-start(s8[16777216]{0:T(1024)(128)(4,1)} %bitcast.119), calls=%async_computation.3 | async-start | bytes 8388608
  137.3 29.0 %slice-start.4 = ((s8[16777216]{0:T(1024)(128)(4,1)}), s8[4194304]{0:T(1024)(128)(4,1)S(1)}, s32[]{:S(2)}) async-start(s8[16777216]{0:T(1024)(128)(4,1)} %bitcast.119), calls=%async_computation.4 | async-start | bytes 8388608
  137.3 29.0 %slice-start.5 = ((s8[16777216]{0:T(1024)(128)(4,1)}), s8[4194304]{0:T(1024)(128)(4,1)S(1)}, s32[]{:S(2)}) async-start(s8[16777216]{0:T(1024)(128)(4,1)} %bitcast.119), calls=%async_computation.5 | async-start | bytes 8388608
  148.7 17.6 %slice-start.6 = ((s8[16777216]{0:T(1024)(128)(4,1)}), s8[4194304]{0:T(1024)(128)(4,1)S(1)}, s32[]{:S(2)}) async-start(s8[16777216]{0:T(1024)(128)(4,1)} %bitcast.119), calls=%async_computation.6 | async-start | bytes 8388608
  162.0 31.4 %slice-start.7 = ((s8[6291456]{0:T(1024)(128)(4,1)}), s8[4194304]{0:T(1024)(128)(4,1)S(1)}, s32[]{:S(2)}) async-start(s8[6291456]{0:T(1024)(128)(4,1)} %bitcast.125), calls=%async_computation.7 | async-start | bytes 8388608
  164.8 28.6 %slice-start.8 = ((s8[6291456]{0:T(1024)(128)(4,1)}), s8[2097152]{0:T(1024)(128)(4,1)S(1)}, s32[]{:S(2)}) async-start(s8[6291456]{0:T(1024)(128)(4,1)} %bitcast.125), calls=%async_computation.8 | async-start | bytes 4194304
  164.8 23.9 %collective-permute-start.4 = (f32[2,8,128,128]{2,3,0,1:T(8,128)}, f32[2,8,128,128]{2,3,0,1:T(8,128)}, u32[]{:S(2)}, u32[]{:S(2)}) collective-permute-start(f32[2,8,128,128]{2,3,0,1:T(8,128)} %slice_add_fusion), channel_id=1, source_target_pairs={{0,8},{8,0},{4,12},{12,4},{16,24},{24,16},{20,28},{28,20},{1,9},{9... | collective-permute-start | bytes 3145736 | tf_op jit(solution)/shard_map/ppermute | solution.py:20
  190.0 36.7 %collective-permute-start.5 = (f32[1,8,128,128]{2,3,0,1:T(8,128)S(1)}, f32[1,8,128,128]{2,3,0,1:T(8,128)}, u32[]{:S(2)}, u32[]{:S(2)}) collective-permute-start(f32[1,8,128,128]{2,3,0,1:T(8,128)S(1)} %slice_add_fusion.1), channel_id=1, source_target_pairs={{0,16},{16,0},{4,20},{20,4},{8,24},{24,8},{12,28},{28,12},{1,17},{... | collective-permute-start | bytes 1572872 | tf_op jit(solution)/shard_map/ppermute | solution.py:20
where the time goes:
time: 246 us; the launch traced here: 245 us
  matrix products  90.1 us (37%)
  waiting for transfers between devices  41.6 us (17%)
  local copies, waits for them, and re-layouts  38.8 us (16%)
  blocking collectives  32.7 us (13%)
  other arithmetic  27.4 us (11%)
  starting transfers between devices  13.7 us (6%)
    ppermute x6, waiting for transfers between devices, from_partner(): return lax.ppermute(block, axis, route)  41.6 us
    unnamed x41, local copies, waits for them, and re-layouts  26.4 us
    psum x1, blocking collectives, body(): grad_gain = lax.psum(jnp.sum(cot_three * normed, axis=0).reshape(-1), 'seq')  20.6 us
    ppermute x6, starting transfers between devices, from_partner(): return lax.ppermute(block, axis, route)  13.7 us
    dot_general x1, matrix products, body(): jnp.einsum('hts,she->the', kept, v_three, preferred_element_type=f32)  12.1 us
    dot_general x1, matrix products, body(): jnp.einsum('hts,she->the', pair, k_three, preferred_element_type=f32)  11.4 us
    dot_general x1, matrix products, body(): jnp.einsum('hts,the->she', kept, weighted, preferred_element_type=f32)  10.9 us
    dot_general x1, matrix products, body(): jnp.einsum('the,she->hts', q_three, k_three, preferred_element_type=f32)  10.4 us
  transfers between devices with their start and end apart: 6, of which 5 were waited for; matrix products, arithmetic and copies ran while one was open for 30% of the time, Pallas kernels for 0%

commit v1 on v0

v1 whole, which is shorter than its diff:
```python
import functools

import jax
import jax.numpy as jnp
from jax import lax
from jax.experimental import pallas as pl
from jax.experimental.pallas import tpu as pltpu
from jax.sharding import PartitionSpec as P

EPS = 1e-06
F32 = jnp.float32
BF16 = jnp.bfloat16
TILE = 256


def dot(left, right, left_dim, right_dim):
    return lax.dot_general(
        left, right, (((left_dim,), (right_dim,)), ((), ())), preferred_element_type=F32
    )


def lane_sums(block):
    high = block.astype(BF16)
    low = (block - high.astype(F32)).astype(BF16)
    ones = jnp.ones((8, 2 * block.shape[1]), BF16)
    return dot(ones, jnp.concatenate([high, low], axis=1), 1, 1)


def level_columns(coef_ref, head):
    rows = [coef_ref[level, pl.ds(head, 1), :] for level in range(coef_ref.shape[0])]
    rows += [jnp.zeros_like(rows[0])] * (8 - len(rows))
    return jnp.concatenate(rows, axis=0).T


def states_kernel(key_ref, value_ref, out_ref):
    out_ref[0] = dot(key_ref[...], value_ref[...], 0, 0)


def local_kernel(query_ref, key_ref, value_ref, out_ref):
    rows = query_ref.shape[0]
    tile = min(TILE, rows)
    keep = lax.broadcasted_iota(jnp.int32, (tile, tile), 0) >= lax.broadcasted_iota(
        jnp.int32, (tile, tile), 1
    )
    for start in range(0, rows, tile):
        here = query_ref[start : start + tile, :]
        edge = jnp.where(keep, dot(here, key_ref[start : start + tile, :], 1, 1), 0.0)
        total = dot(edge.astype(BF16), value_ref[start : start + tile, :], 1, 0)
        if start:
            full = dot(here, key_ref[:start, :], 1, 1).astype(BF16)
            total += dot(full, value_ref[:start, :], 1, 0)
        out_ref[start : start + tile, :] = total


def output_kernel(
    bits_ref, query_ref, local_ref, cot_ref, gain_ref, coef_ref, *refs
):
    bucket_refs, (out_ref, sums_ref, square_ref, inner_ref) = refs[:-4], refs[-4:]
    head = pl.program_id(0)
    rows = query_ref.shape[0]
    tile = min(TILE, rows)
    columns = level_columns(coef_ref, head)
    width = query_ref.shape[1]
    halves = [
        (ref[0] * bits_ref[level]).astype(BF16) for level, ref in enumerate(bucket_refs)
    ]
    wide = jnp.concatenate(halves, axis=1)

    @pl.when(head == 0)
    def _():
        square_ref[...] = jnp.zeros_like(square_ref)
        inner_ref[...] = jnp.zeros_like(inner_ref)

    for start in range(0, rows, tile):
        span = slice(start, start + tile)
        reads = dot(query_ref[span, :], wide, 1, 0)
        out = columns[span, 0:1] * local_ref[span, :]
        for level in range(len(halves)):
            out += columns[span, level + 1 : level + 2] * reads[:, level * width : (level + 1) * width]
        out_ref[span, :] = out
        weighted = cot_ref[span, :].astype(F32) * gain_ref[...]
        square_ref[span, :] += out * out
        inner_ref[span, :] += weighted * out

    @pl.when(head == pl.num_programs(0) - 1)
    def _():
        sums_ref[0:8, :] = lane_sums(square_ref[...])
        sums_ref[8:16, :] = lane_sums(inner_ref[...])


def grad_output(cot, gain, out, inverse, factor):
    return ((cot * gain - out * factor) * inverse).astype(BF16)


def bucket_kernel(
    bits_ref, query_ref, out_ref, cot_ref, gain_ref, coef_ref, stats_ref, *refs
):
    bucket_refs, (half_ref, gain_out_ref) = refs[:-2], refs[-2:]
    head = pl.program_id(0)
    rows = query_ref.shape[0]
    tile = min(TILE, rows)
    columns = level_columns(coef_ref, head)
    stats = stats_ref[...].T
    totals = [None] * len(bucket_refs)
    gain_total = None
    for start in range(0, rows, tile):
        span = slice(start, start + tile)
        inverse = stats[span, 0:1]
        out = out_ref[span, :]
        cot = cot_ref[span, :].astype(F32)
        part = jnp.sum(cot * (out * inverse), axis=0, keepdims=True)
        gain_total = part if gain_total is None else gain_total + part
        half = grad_output(cot, gain_ref[...], out, inverse, stats[span, 1:2])
        half_ref[span, :] = half
        wide = half.astype(F32)
        scaled = jnp.concatenate(
            [
                (columns[span, level + 1 : level + 2] * wide).astype(BF16)
                for level in range(len(bucket_refs))
            ],
            axis=1,
        )
        part = dot(query_ref[span, :], scaled, 0, 0)
        totals = part if totals[0] is None else totals + part
    width = query_ref.shape[1]
    for level, ref in enumerate(bucket_refs):
        ref[0] = totals[:, level * width : (level + 1) * width] * bits_ref[level]
    gain_out_ref[...] = gain_total[None]


def main_kernel(
    bits_ref,
    query_ref,
    key_ref,
    value_ref,
    local_ref,
    out_ref,
    half_ref,
    gain_ref,
    coef_ref,
    stats_ref,
    *refs,
):
    count = coef_ref.shape[0] - 1
    bucket_refs = refs[:count]
    mixed_ref, grad_query_ref, key_sum_ref, value_sum_ref, level_ref, query_sum_ref = refs[count:]
    head = pl.program_id(0)
    rows, width = query_ref.shape
    tile = min(TILE, rows)
    columns = level_columns(coef_ref, head)
    first_row = coef_ref[0, pl.ds(head, 1), :]
    stats = stats_ref[...].T
    halves = [
        (ref[0] * bits_ref[level]).astype(BF16) for level, ref in enumerate(bucket_refs)
    ]
    wide = jnp.concatenate(halves, axis=1)
    for start in range(0, rows, tile):
        span = slice(start, start + tile)
        mixed_ref[span, :] = (out_ref[span, :] * stats[span, 0:1] * gain_ref[...]).astype(BF16)
        grad = half_ref[span, :].astype(F32)
        reads = dot(query_ref[span, :], wide, 1, 0)
        level_ref[0, pl.ds(head, 1), span] = lane_sums(grad * local_ref[span, :])[0:1]
        for level in range(count):
            read = reads[:, level * width : (level + 1) * width]
            level_ref[level + 1, pl.ds(head, 1), span] = lane_sums(grad * read)[0:1]
        scaled = jnp.concatenate(
            [
                (columns[span, level + 1 : level + 2] * grad).astype(BF16)
                for level in range(count)
            ],
            axis=1,
        )
        query_sum_ref[span, :] = dot(scaled, wide, 1, 1)
    weighted = (columns[:, 0:1] * half_ref[...].astype(F32)).astype(BF16)
    keep = lax.broadcasted_iota(jnp.int32, (tile, tile), 0) <= lax.broadcasted_iota(
        jnp.int32, (tile, tile), 1
    )
    for start in range(0, rows, tile):
        span = slice(start, start + tile)
        key = key_ref[span, :]
        value = value_ref[span, :]
        key_sum = None
        value_sum = None
        for low, high in ((start, start + tile), (start + tile, rows)):
            if low >= high:
                continue
            later = slice(low, high)
            scores = dot(key, query_ref[later, :], 1, 1)
            pair = dot(value, half_ref[later, :], 1, 1) * first_row[:, later]
            if low == start:
                scores = jnp.where(keep, scores, 0.0)
                pair = jnp.where(keep, pair, 0.0)
            scores = scores.astype(BF16)
            pair = pair.astype(BF16)
            value_part = dot(scores, weighted[later, :], 1, 0)
            key_part = dot(pair, query_ref[later, :], 1, 0)
            value_sum = value_part if value_sum is None else value_sum + value_part
            key_sum = key_part if key_sum is None else key_sum + key_part
            query_sum_ref[later, :] += dot(pair, key, 0, 0)
        key_sum_ref[span, :] = key_sum
        value_sum_ref[span, :] = value_sum
    grad_query_ref[...] = query_sum_ref[...].astype(BF16)


def final_kernel(key_ref, value_ref, key_sum_ref, value_sum_ref, state_ref, key_out_ref, value_out_ref):
    state = state_ref[0].astype(BF16)
    key_out_ref[...] = (key_sum_ref[...] + dot(value_ref[...], state, 1, 1)).astype(BF16)
    value_out_ref[...] = (value_sum_ref[...] + dot(key_ref[...], state, 1, 0)).astype(BF16)


def exchange(block, apart, count, direction=None):
    mask = 1 << apart
    route = [(low, low ^ mask) for low in range(count)]
    if direction == "up":
        route = [pair for pair in route if not pair[0] & mask]
    if direction == "down":
        route = [pair for pair in route if pair[0] & mask]
    return lax.ppermute(block, "seq", route)


def body(seq_count, heads_all, query, key, value, level_coef, gain, cotangent):
    rows = query.shape[0]
    heads = level_coef.shape[1]
    width = query.shape[1] // heads
    depth = level_coef.shape[0] - 1
    features = heads_all * query.shape[1]
    group = lax.axis_index("seq")
    bits = jnp.stack([(group // 2**level % 2).astype(F32) for level in range(depth)])
    gain_row = gain.reshape(1, -1)

    smem = pl.BlockSpec(memory_space=pltpu.SMEM)
    token = pl.BlockSpec((rows, width), lambda h: (0, h))
    state = pl.BlockSpec((1, width, width), lambda h: (h, 0, 0))
    gain_spec = pl.BlockSpec((1, width), lambda h: (0, h))
    coef_spec = pl.BlockSpec(level_coef.shape, lambda h: (0, 0, 0))
    stats_spec = pl.BlockSpec((8, rows), lambda h: (0, 0))
    token_f32 = jax.ShapeDtypeStruct((rows, heads * width), F32)
    token_bf16 = jax.ShapeDtypeStruct((rows, heads * width), BF16)
    state_f32 = jax.ShapeDtypeStruct((heads, width, width), F32)
    params = pltpu.CompilerParams(dimension_semantics=("arbitrary",))
    square = rows * width * width * heads

    def call(kernel, name, flops, moved, **keys):
        return pl.pallas_call(
            kernel,
            grid=(heads,),
            name=name,
            compiler_params=params,
            cost_estimate=pl.CostEstimate(flops=flops, bytes_accessed=moved, transcendentals=0),
            **keys,
        )

    size = rows * heads * width
    states = call(
        states_kernel,
        "states",
        2 * square,
        4 * size,
        in_specs=[token, token],
        out_specs=state,
        out_shape=state_f32,
    )(key, value)

    local = call(
        local_kernel,
        "local",
        3 * rows * size,
        10 * size,
        in_specs=[token, token, token],
        out_specs=token,
        out_shape=token_f32,
    )(query, key, value)

    block = states
    buckets = []
    for level in range(depth):
        last = level == depth - 1
        other = exchange(block, level, seq_count, "up" if last else None)
        buckets.append(other)
        if not last:
            block = block + other

    output, sums = call(
        output_kernel,
        "output",
        2 * depth * square,
        12 * size,
        in_specs=[smem, token, token, token, gain_spec, coef_spec] + [state] * depth,
        out_specs=[token, pl.BlockSpec((16, rows), lambda h: (0, 0))],
        out_shape=[token_f32, jax.ShapeDtypeStruct((16, rows), F32)],
        scratch_shapes=[pltpu.VMEM((rows, width), F32)] * 2,
    )(bits, query, local, cotangent, gain_row, level_coef, *buckets)

    total = lax.psum(jnp.stack([sums[0], sums[8]]), "head")
    inverse = lax.rsqrt(total[0] / features + EPS)
    factor = total[1] * inverse * inverse / features
    stats = jnp.concatenate([inverse[None], factor[None], jnp.zeros((6, rows), F32)])

    grads = call(
        bucket_kernel,
        "buckets",
        2 * depth * square,
        10 * size,
        in_specs=[smem, token, token, token, gain_spec, coef_spec, stats_spec],
        out_specs=[state] * depth
        + [token, pl.BlockSpec((1, 1, width), lambda h: (h, 0, 0))],
        out_shape=[state_f32] * depth
        + [token_bf16, jax.ShapeDtypeStruct((heads, 1, width), F32)],
    )(bits, query, output, cotangent, gain_row, level_coef, stats)
    grad_buckets, half, gain_part = grads[:depth], grads[depth], grads[depth + 1]

    carried = None
    for level in reversed(range(depth)):
        if carried is None:
            carried = exchange(grad_buckets[level], level, seq_count, "down")
        else:
            carried = carried + exchange(grad_buckets[level] + carried, level, seq_count)

    grad_gain = gain_part.reshape(-1)
    for level in range(depth):
        grad_gain = grad_gain + exchange(grad_gain, level, seq_count)

    mixed, grad_query, key_sum, value_sum, grad_level = call(
        main_kernel,
        "main",
        8 * rows * size + 4 * depth * square,
        26 * size,
        in_specs=[smem, token, token, token, token, token, token, gain_spec, coef_spec, stats_spec]
        + [state] * depth,
        out_specs=[token, token, token, token, coef_spec],
        out_shape=[
            token_bf16,
            token_bf16,
            token_f32,
            token_f32,
            jax.ShapeDtypeStruct(level_coef.shape, F32),
        ],
        scratch_shapes=[pltpu.VMEM((rows, width), F32)],
    )(bits, query, key, value, local, output, half, gain_row, level_coef, stats, *buckets)

    grad_key, grad_value = call(
        final_kernel,
        "final",
        4 * square,
        16 * size,
        in_specs=[token, token, token, token, state],
        out_specs=[token, token],
        out_shape=[token_bf16, token_bf16],
    )(key, value, key_sum, value_sum, carried)
    return (mixed, grad_query, grad_key, grad_value, grad_level, grad_gain)


def solution(mesh):
    placed = (
        P("seq", "head"),
        P("seq", "head"),
        P("seq", "head"),
        P(None, "head", "seq"),
        P("head"),
        P("seq", "head"),
    )
    return jax.shard_map(
        functools.partial(body, mesh.shape["seq"], mesh.shape["head"]),
        mesh=mesh,
        in_specs=placed,
        out_specs=(
            P("seq", "head"),
            P("seq", "head"),
            P("seq", "head"),
            P("seq", "head"),
            P(None, "head", "seq"),
            P("head"),
        ),
        check_vma=False,
    )
```

time: 246 us -> 179 us (0.73)
  matrix products: 90.1 us -> 0 us
  Pallas kernels: 0 us -> 88 us
  local copies, waits for them, and re-layouts: 38.8 us -> 1.65 us
  blocking collectives: 32.7 us -> 5.77 us
  other arithmetic: 27.4 us -> 7.09 us
  waiting for transfers between devices: 41.6 us -> 58.7 us
    dot_general x12 -> x0, matrix products: 90.1 us -> none  [the longest x1 12.1 us: body(): jnp.einsum('hts,she->the', kept, v_three, preferred_element_type=f32)]
    pallas_call x0 -> x6, Pallas kernels: none -> 88 us  [the longest x1 35.4 us: body(): call(main_kernel, 'main', 8 * rows * size + 4 * depth * square, 26 * size...]
    psum x3 -> x1, blocking collectives: 32.7 us -> 5.77 us  [body(): total = lax.psum(jnp.stack([sums[0], sums[8]]), 'head')]
    unnamed x41 -> x6, local copies, waits for them, and re-layouts: 26.4 us -> 0.8 us
    ppermute x6 -> x9, waiting for transfers between devices: 41.6 us -> 58.7 us  [exchange(): return lax.ppermute(block, 'seq', route)]
    reduce_sum x3 -> x0, other arithmetic: 16.7 us -> none  [the longest x1 6.69 us: body(): grad_first = jnp.sum(grad_float * local, axis=-1)]
    reshape x2 -> x0, local copies, waits for them, and re-layouts: 8.19 us -> none  [the longest x1 4.1 us: body(): k_three = key.reshape(rows, heads_here, width)]
    convert_element_type x1 -> x0, local copies, waits for them, and re-layouts: 4.12 us -> none  [body(): cot_three = cotangent.reshape(rows, heads_here, width).astype(f32)]
  transfers between devices with their start and end apart: 6 -> 9, of which waited for: 5 -> 5; matrix products, arithmetic and copies ran while one was open for 30% -> 2% of each run, Pallas kernels for 0% -> 26%
where the time goes in v1:
time: 179 us; the launch traced here: 178 us
  Pallas kernels  88 us (49%)
  waiting for transfers between devices  58.7 us (33%)
  starting transfers between devices  15.9 us (9%)
  other arithmetic  7.09 us (4%)
  blocking collectives  5.77 us (3%)
    ppermute x9, waiting for transfers between devices, exchange(): return lax.ppermute(block, 'seq', route)  58.7 us
    pallas_call x1, Pallas kernels, body(): call(main_kernel, 'main', 8 * rows * size + 4 * depth * square, 26 * size...  35.4 us
    ppermute x9, starting transfers between devices, exchange(): return lax.ppermute(block, 'seq', route)  15.9 us
    pallas_call x1, Pallas kernels, body(): call(bucket_kernel, 'buckets', 2 * depth * square, 10 * size, in_specs=[s...  13.1 us
    pallas_call x1, Pallas kernels, body(): call(output_kernel, 'output', 2 * depth * square, 12 * size, in_specs=[sm...  12.1 us
    pallas_call x1, Pallas kernels, body(): call(local_kernel, 'local', 3 * rows * size, 10 * size, in_specs=[token,...  11.4 us
    pallas_call x1, Pallas kernels, body(): call(final_kernel, 'final', 4 * square, 16 * size, in_specs=[token, token...  9.32 us
    pallas_call x1, Pallas kernels, body(): call(states_kernel, 'states', 2 * square, 4 * size, in_specs=[token, toke...  6.67 us
  transfers between devices with their start and end apart: 9, of which 5 were waited for; matrix products, arithmetic and copies ran while one was open for 2% of the time, Pallas kernels for 26%

profile of v1, /device:TPU:0, one launch (start us, length us, event | category | flops | bytes accessed | tf_op | source)
XLA Modules:
  0.0 177.8 jit_solution(3826723890382222055)
XLA Ops:
  0.6 6.7 %states.1 = f32[8,128,128]{2,1,0:T(8,128)} custom-call(bf16[1024,1024]{1,0:T(8,128)(2,1)} %key_ref.7, bf16[1024,1024]{1,0:T(8,128)(2,1)} %value_ref.7), custom_call_target="tpu_custom_call" | custom-call | flops 268435456 | bytes 4194304 | tf_op jit(solution)/shard_map/states/pallas_call | solution.py:254
  7.3 3.0 %collective-permute-start = (f32[8,128,128]{2,1,0:T(8,128)}, f32[8,128,128]{2,1,0:T(8,128)S(1)}, u32[]{:S(2)}, u32[]{:S(2)}) collective-permute-start(f32[8,128,128]{2,1,0:T(8,128)} %states.1), channel_id=1, source_target_pairs={{0,4},{4,0},{8,12},{12,8},{16,20},{20,16},{24,28},{28,24},{1,5},{5... | collective-permute-start | bytes 1572872 | tf_op jit(solution)/shard_map/ppermute | solution.py:218
  10.3 12.1 %collective-permute-done.refs_0_ = f32[8,128,128]{2,1,0:T(8,128)S(1)} collective-permute-done((f32[8,128,128]{2,1,0:T(8,128)}, f32[8,128,128]{2,1,0:T(8,128)S(1)}, u32[]{:S(2)}, u32[]{:S(2)}) %collective-permute-start) | collective-permute-done | bytes 524320 | tf_op jit(solution)/shard_map/ppermute | solution.py:218
  22.4 1.3 add.53
  23.7 1.9 %collective-permute-start.1 = (f32[8,128,128]{2,1,0:T(8,128)S(1)}, f32[8,128,128]{2,1,0:T(8,128)S(1)}, u32[]{:S(2)}, u32[]{:S(2)}) collective-permute-start(f32[8,128,128]{2,1,0:T(8,128)S(1)} %add.53), channel_id=1, source_target_pairs={{0,8},{4,12},{8,0},{12,4},{16,24},{20,28},{24,16},{28,20},{1,9},{5... | collective-permute-start | bytes 1572872 | tf_op jit(solution)/shard_map/ppermute | solution.py:218
  25.6 11.3 %collective-permute-done.1.refs_1_ = f32[8,128,128]{2,1,0:T(8,128)S(1)} collective-permute-done((f32[8,128,128]{2,1,0:T(8,128)S(1)}, f32[8,128,128]{2,1,0:T(8,128)S(1)}, u32[]{:S(2)}, u32[]{:S(2)}) %collective-permute-start.1) | collective-permute-done | bytes 524320 | tf_op jit(solution)/shard_map/ppermute | solution.py:218
  36.9 0.1 add.54
  37.0 4.5 %collective-permute-start.2 = (f32[8,128,128]{2,1,0:T(8,128)S(1)}, f32[8,128,128]{2,1,0:T(8,128)S(1)}, u32[]{:S(2)}, u32[]{:S(2)}) collective-permute-start(f32[8,128,128]{2,1,0:T(8,128)S(1)} %add.54), channel_id=1, source_target_pairs={{0,16},{4,20},{8,24},{12,28},{1,17},{5,21},{9,25},{13,29},{2,18},{... | collective-permute-start | bytes 1572872 | tf_op jit(solution)/shard_map/ppermute | solution.py:218
  41.5 0.1 pad.2.clone
  41.6 0.6 pad_maximum_fusion.1.bits_ref
  42.2 11.4 %local.1.local_ref = f32[1024,1024]{1,0:T(8,128)} custom-call(bf16[1024,1024]{1,0:T(8,128)(2,1)} %query_ref.7, bf16[1024,1024]{1,0:T(8,128)(2,1)} %key_ref.7, bf16[1024,1024]{1,0:T(8,128)(2,1)} %value_ref.7), custom_call_target="tpu_custom_call" | custom-call | flops 3221225472 | bytes 10485760 | tf_op jit(solution)/shard_map/local/pallas_call | solution.py:264
  53.6 0.8 copy-done.2
  54.4 12.1 %output.1 = (f32[1024,1024]{1,0:T(8,128)}, f32[16,1024]{1,0:T(8,128)}) custom-call(f32[3]{0:T(128)} %pad_maximum_fusion.1.bits_ref, bf16[1024,1024]{1,0:T(8,128)(2,1)} %query_ref.7, f32[1024,1024]{1,0:T(8,128)} %local.1.local_ref, bf16[1024,1024]{1,0:T(8,128)(2,1)} %cot_ref.3, f32[1,1024]{1,0:T(1,128)} %bitcast.5, f32[4,8,1024]{2,1,0:T(8,128)} %coef_ref.5, ...), custom_call_target="tpu_custom_call" | custom-call | flops 805306368 | bytes 12582912 | tf_op jit(solution)/shard_map/output/pallas_call | solution.py:283
  66.5 0.8 fusion.5
  67.3 5.8 %psum.7 = f32[2,1024]{1,0:T(2,128)S(1)} all-reduce(f32[2,1024]{1,0:T(2,128)S(1)} %pad_maximum_fusion), channel_id=1, replica_groups=mesh['seq'=8,'head'=4] {'head'}, use_global_device_ids=true, to_apply=%region_0.1 | all-reduce | flops 2048 | bytes 16384 | tf_op jit(solution)/shard_map/psum | solution.py:294
  73.1 0.7 maximum_maximum_fusion.stats_ref
  73.7 13.1 %buckets.1 = (f32[8,128,128]{2,1,0:T(8,128)}, f32[8,128,128]{2,1,0:T(8,128)}, f32[8,128,128]{2,1,0:T(8,128)}, bf16[1024,1024]{1,0:T(8,128)(2,1)}, f32[8,1,128]{2,1,0:T(1,128)}) custom-call(f32[3]{0:T(128)} %pad_maximum_fusion.1.bits_ref, bf16[1024,1024]{1,0:T(8,128)(2,1)} %query_ref.7, f32[1024,1024]{1,0:T(8,128)} %get-tuple-element.20.out_ref, ...), custom_call_target="tpu_custom_call" | custom-call | flops 805306368 | bytes 10485760 | tf_op jit(solution)/shard_map/buckets/pallas_call | solution.py:299
  86.8 1.3 collective-permute-start.3
  88.1 26.6 %collective-permute-done.3 = f32[8,128,128]{2,1,0:T(8,128)S(1)} collective-permute-done((f32[8,128,128]{2,1,0:T(8,128)}, f32[8,128,128]{2,1,0:T(8,128)S(1)}, u32[]{:S(2)}, u32[]{:S(2)}) %collective-permute-start.3) | collective-permute-done | bytes 524320 | tf_op jit(solution)/shard_map/ppermute | solution.py:218
  114.7 1.1 add.57
  115.8 0.1 collective-permute-start.4
  115.9 1.6 collective-permute-start.6
  117.5 2.3 %collective-permute-done.6 = f32[1024]{0:T(1024)S(1)} collective-permute-done((f32[1024]{0:T(1024)}, f32[1024]{0:T(1024)S(1)}, u32[]{:S(2)}, u32[]{:S(2)}) %collective-permute-start.6) | collective-permute-done | bytes 4128 | tf_op jit(solution)/shard_map/ppermute | solution.py:218
  119.8 0.7 add.61
  120.5 1.9 %collective-permute-start.7 = (f32[1024]{0:T(1024)S(1)}, f32[1024]{0:T(1024)S(1)}, u32[]{:S(2)}, u32[]{:S(2)}) collective-permute-start(f32[1024]{0:T(1024)S(1)} %add.61), channel_id=1, source_target_pairs={{0,8},{4,12},{8,0},{12,4},{16,24},{20,28},{24,16},{28,20},{1,9},{5... | collective-permute-start | bytes 12296 | tf_op jit(solution)/shard_map/ppermute | solution.py:218
  122.4 6.4 %collective-permute-done.7 = f32[1024]{0:T(1024)S(1)} collective-permute-done((f32[1024]{0:T(1024)S(1)}, f32[1024]{0:T(1024)S(1)}, u32[]{:S(2)}, u32[]{:S(2)}) %collective-permute-start.7) | collective-permute-done | bytes 4128 | tf_op jit(solution)/shard_map/ppermute | solution.py:218
  128.8 1.1 fusion.3
  130.0 1.6 collective-permute-start.5
  131.6 35.4 %main.1 = (bf16[1024,1024]{1,0:T(8,128)(2,1)}, bf16[1024,1024]{1,0:T(8,128)(2,1)}, f32[1024,1024]{1,0:T(8,128)}, f32[1024,1024]{1,0:T(8,128)}, f32[4,8,1024]{2,1,0:T(8,128)}) custom-call(f32[3]{0:T(128)} %pad_maximum_fusion.1.bits_ref, bf16[1024,1024]{1,0:T(8,128)(2,1)} %query_ref.7, bf16[1024,1024]{1,0:T(8,128)(2,1)} %key_ref.7, ...), custom_call_target="tpu_custom_call" | custom-call | flops 10200547328 | bytes 27262976 | tf_op jit(solution)/shard_map/main/pallas_call | solution.py:323
  167.0 0.6 add.63
  167.6 0.9 add.60.state_ref
  168.5 9.3 %final.1 = (bf16[1024,1024]{1,0:T(8,128)(2,1)}, bf16[1024,1024]{1,0:T(8,128)(2,1)}) custom-call(bf16[1024,1024]{1,0:T(8,128)(2,1)} %key_ref.7, bf16[1024,1024]{1,0:T(8,128)(2,1)} %value_ref.7, f32[1024,1024]{1,0:T(8,128)} %get-tuple-element.25.key_sum_ref, f32[1024,1024]{1,0:T(8,128)} %get-tuple-element.26.value_sum_ref, f32[8,128,128]{2,1,0:T(8,128)} %add.60.state_ref), custom_call_target="tpu_custom_call" | custom-call | flops 536870912 | bytes 16777216 | tf_op jit(solution)/shard_map/final/pallas_call | solution.py:341
  (14 shorter events, 0.1 us)
Async XLA Ops:
  7.3 15.1 %collective-permute-start = (f32[8,128,128]{2,1,0:T(8,128)}, f32[8,128,128]{2,1,0:T(8,128)S(1)}, u32[]{:S(2)}, u32[]{:S(2)}) collective-permute-start(f32[8,128,128]{2,1,0:T(8,128)} %states.1), channel_id=1, source_target_pairs={{0,4},{4,0},{8,12},{12,8},{16,20},{20,16},{24,28},{28,24},{1,5},{5... | collective-permute-start | bytes 1572872 | tf_op jit(solution)/shard_map/ppermute | solution.py:218
  22.4 31.1 %copy-start = (f32[8,128,128]{2,1,0:T(8,128)}, f32[8,128,128]{2,1,0:T(8,128)S(1)}, u32[]{:S(2)}) copy-start(f32[8,128,128]{2,1,0:T(8,128)S(1)} %collective-permute-done.refs_0_) | copy-start | bytes 1572868
  23.7 13.2 %collective-permute-start.1 = (f32[8,128,128]{2,1,0:T(8,128)S(1)}, f32[8,128,128]{2,1,0:T(8,128)S(1)}, u32[]{:S(2)}, u32[]{:S(2)}) collective-permute-start(f32[8,128,128]{2,1,0:T(8,128)S(1)} %add.53), channel_id=1, source_target_pairs={{0,8},{4,12},{8,0},{12,4},{16,24},{20,28},{24,16},{28,20},{1,9},{5... | collective-permute-start | bytes 1572872 | tf_op jit(solution)/shard_map/ppermute | solution.py:218
  36.9 16.7 %copy-start.1 = (f32[8,128,128]{2,1,0:T(8,128)}, f32[8,128,128]{2,1,0:T(8,128)S(1)}, u32[]{:S(2)}) copy-start(f32[8,128,128]{2,1,0:T(8,128)S(1)} %collective-permute-done.1.refs_1_) | copy-start | bytes 1572868
  37.0 16.6 %collective-permute-start.2 = (f32[8,128,128]{2,1,0:T(8,128)S(1)}, f32[8,128,128]{2,1,0:T(8,128)S(1)}, u32[]{:S(2)}, u32[]{:S(2)}) collective-permute-start(f32[8,128,128]{2,1,0:T(8,128)S(1)} %add.54), channel_id=1, source_target_pairs={{0,16},{4,20},{8,24},{12,28},{1,17},{5,21},{9,25},{13,29},{2,18},{... | collective-permute-start | bytes 1572872 | tf_op jit(solution)/shard_map/ppermute | solution.py:218
  53.6 0.8 copy-start.2
  86.8 27.9 %collective-permute-start.3 = (f32[8,128,128]{2,1,0:T(8,128)}, f32[8,128,128]{2,1,0:T(8,128)S(1)}, u32[]{:S(2)}, u32[]{:S(2)}) collective-permute-start(f32[8,128,128]{2,1,0:T(8,128)} %get-tuple-element.27), channel_id=1, source_target_pairs={{16,0},{20,4},{24,8},{28,12},{17,1},{21,5},{25,9},{29,13},{18,2},{... | collective-permute-start | bytes 1572872 | tf_op jit(solution)/shard_map/ppermute | solution.py:218
  115.8 13.0 %collective-permute-start.4 = (f32[8,128,128]{2,1,0:T(8,128)S(1)}, f32[8,128,128]{2,1,0:T(8,128)S(1)}, u32[]{:S(2)}, u32[]{:S(2)}) collective-permute-start(f32[8,128,128]{2,1,0:T(8,128)S(1)} %add.57), channel_id=1, source_target_pairs={{0,8},{4,12},{8,0},{12,4},{16,24},{20,28},{24,16},{28,20},{1,9},{5... | collective-permute-start | bytes 1572872 | tf_op jit(solution)/shard_map/ppermute | solution.py:218
  115.9 3.9 %collective-permute-start.6 = (f32[1024]{0:T(1024)}, f32[1024]{0:T(1024)S(1)}, u32[]{:S(2)}, u32[]{:S(2)}) collective-permute-start(f32[1024]{0:T(1024)} %bitcast.8), channel_id=1, source_target_pairs={{0,4},{4,0},{8,12},{12,8},{16,20},{20,16},{24,28},{28,24},{1,5},{5... | collective-permute-start | bytes 12296 | tf_op jit(solution)/shard_map/ppermute | solution.py:218
  120.5 8.3 %collective-permute-start.7 = (f32[1024]{0:T(1024)S(1)}, f32[1024]{0:T(1024)S(1)}, u32[]{:S(2)}, u32[]{:S(2)}) collective-permute-start(f32[1024]{0:T(1024)S(1)} %add.61), channel_id=1, source_target_pairs={{0,8},{4,12},{8,0},{12,4},{16,24},{20,28},{24,16},{28,20},{1,9},{5... | collective-permute-start | bytes 12296 | tf_op jit(solution)/shard_map/ppermute | solution.py:218
  128.8 38.2 %collective-permute-start.8 = (f32[1024]{0:T(1024)S(1)}, f32[1024]{0:T(1024)S(1)}, u32[]{:S(2)}, u32[]{:S(2)}) collective-permute-start(f32[1024]{0:T(1024)S(1)} %add.62), channel_id=1, source_target_pairs={{0,16},{4,20},{8,24},{12,28},{16,0},{20,4},{24,8},{28,12},{1,17},{... | collective-permute-start | bytes 12296 | tf_op jit(solution)/shard_map/ppermute | solution.py:218
  130.0 37.7 %collective-permute-start.5 = (f32[8,128,128]{2,1,0:T(8,128)S(1)}, f32[8,128,128]{2,1,0:T(8,128)S(1)}, u32[]{:S(2)}, u32[]{:S(2)}) collective-permute-start(f32[8,128,128]{2,1,0:T(8,128)S(1)} %get-tuple-element.34), channel_id=1, source_target_pairs={{0,4},{4,0},{8,12},{12,8},{16,20},{20,16},{24,28},{28,24},{1,5},{5... | collective-permute-start | bytes 1572872 | tf_op jit(solution)/shard_map/ppermute | solution.py:218

commit v2 on v0

v2 whole, which is shorter than its diff:
```python
import functools

import jax
import jax.numpy as jnp
from jax import lax
from jax.experimental import pallas as pl
from jax.experimental.pallas import tpu as pltpu
from jax.sharding import PartitionSpec as P

EPS = 1e-06
F32 = jnp.float32
BF16 = jnp.bfloat16
TILE = 256
VMEM_LIMIT = 20 * 2**20


def dot(left, right, left_dim, right_dim):
    return lax.dot_general(
        left, right, (((left_dim,), (right_dim,)), ((), ())), preferred_element_type=F32
    )


def lane_sums(block):
    high = block.astype(BF16)
    low = (block - high.astype(F32)).astype(BF16)
    ones = jnp.ones((8, 2 * block.shape[1]), BF16)
    return dot(ones, jnp.concatenate([high, low], axis=1), 1, 1)


def level_columns(coef_ref, head):
    rows = [coef_ref[level, pl.ds(head, 1), :] for level in range(coef_ref.shape[0])]
    rows += [jnp.zeros_like(rows[0])] * (8 - len(rows))
    return jnp.concatenate(rows, axis=0).T


def states_kernel(where_ref, key_ref, value_ref, out_ref):
    out_ref[0] = dot(key_ref[...], value_ref[...], 0, 0)


def local_kernel(where_ref, query_ref, key_ref, value_ref, out_ref):
    rows = query_ref.shape[0]
    tile = min(TILE, rows)
    keep = lax.broadcasted_iota(jnp.int32, (tile, tile), 0) >= lax.broadcasted_iota(
        jnp.int32, (tile, tile), 1
    )
    for start in range(0, rows, tile):
        span = slice(start, start + tile)
        scores = dot(query_ref[start:, :], key_ref[span, :], 1, 1)
        kept = [jnp.where(keep, scores[:tile], 0.0).astype(BF16)]
        if start + tile < rows:
            kept.append(scores[tile:].astype(BF16))
        part = dot(jnp.concatenate(kept, axis=0), value_ref[span, :], 1, 0)
        if start:
            part += out_ref[start:, :]
        out_ref[start:, :] = part


def fill(wide_ref, ref, first, level, bit=None):
    width = ref.shape[1]
    for index in range(ref.shape[0]):
        block = ref[index] if bit is None else ref[index] * bit
        wide_ref[first + index, level * width : (level + 1) * width, :] = block.astype(BF16)


def other_bit(bit, flip):
    return 1 - bit if flip else bit


def output_kernel(where_ref, query_ref, local_ref, cot_ref, gain_ref, coef_ref, *refs):
    bucket_refs, (out_ref, sums_ref, wide_ref) = refs[:-3], refs[-3:]
    heads, _, width = wide_ref.shape
    depth = wide_ref.shape[1] // width

    @pl.when(pl.program_id(0) == 0)
    def _():
        low, high = where_ref[0], where_ref[1]
        half, quarter = heads // 2, heads // 4
        bit = low.astype(F32)
        fill(wide_ref, bucket_refs[0], low * half, 0, bit)
        fill(wide_ref, bucket_refs[1], (1 - low) * half, 0, bit)
        fill(wide_ref, bucket_refs[2], low * half, 1)
        fill(wide_ref, bucket_refs[3], (1 - low) * half, 1)
        for offset in range(4):
            piece = 2 * other_bit(low, offset & 1) + other_bit(high, offset >> 1)
            fill(wide_ref, bucket_refs[4 + offset], piece * quarter, 2)
        for level in range(3, depth):
            fill(wide_ref, bucket_refs[5 + level], 0, level, where_ref[level].astype(F32))

    columns = coef_ref[...].T
    square = None
    for head in range(heads):
        lanes = slice(head * width, (head + 1) * width)
        query = query_ref[:, lanes]
        out = columns[:, head : head + 1] * local_ref[:, lanes]
        for level in range(depth):
            read = dot(query, wide_ref[head, level * width : (level + 1) * width, :], 1, 0)
            place = (level + 1) * heads + head
            out += columns[:, place : place + 1] * read
        out_ref[:, lanes] = out
        weighted = cot_ref[:, lanes].astype(F32) * gain_ref[:, lanes]
        square = out * out if square is None else square + out * out
        inner = weighted * out if head == 0 else inner + weighted * out
    sums_ref[0:1, :] = lane_sums(square)[0:1]
    sums_ref[1:2, :] = lane_sums(inner)[0:1]


def bucket_kernel(features, where_ref, query_ref, out_ref, cot_ref, gain_ref, coef_ref, sums_ref, *refs):
    mixed_ref, half_ref, gain_out_ref = refs[:3]
    mine0_ref, theirs0_ref, mine1_ref, theirs1_ref = refs[3:7]
    quarter_refs, extra_refs, (total_ref, gain_total_ref) = refs[7:11], refs[11:-2], refs[-2:]
    heads, stacked, width = total_ref.shape
    depth = stacked // width
    step = pl.program_id(0)
    tile = query_ref.shape[0]

    @pl.when(step == 0)
    def _():
        total_ref[...] = jnp.zeros_like(total_ref)
        gain_total_ref[...] = jnp.zeros_like(gain_total_ref)

    inverse = lax.rsqrt(sums_ref[0:1, :] / features + EPS)
    factor = sums_ref[1:2, :] * inverse * inverse / features
    columns = jnp.concatenate([inverse, factor, jnp.zeros((6, tile), F32)]).T
    inverse = jnp.broadcast_to(columns[:, 0:1], (tile, width))
    factor = jnp.broadcast_to(columns[:, 1:2], (tile, width))
    for head in range(heads):
        lanes = slice(head * width, (head + 1) * width)
        cot = cot_ref[:, lanes].astype(F32)
        normed = out_ref[:, lanes] * inverse
        gain = gain_ref[:, lanes]
        mixed_ref[:, lanes] = (normed * gain).astype(BF16)
        gain_total_ref[head] += jnp.sum((cot * normed).reshape(tile // 8, 8, width), axis=0)
        half = ((cot * gain) * inverse - normed * factor).astype(BF16)
        half_ref[:, lanes] = half
        turned = query_ref[:, lanes].T.astype(F32)
        stack = jnp.concatenate(
            [
                (turned * coef_ref[(level + 1) * heads + head : (level + 1) * heads + head + 1, :]).astype(BF16)
                for level in range(depth)
            ],
            axis=0,
        )
        total_ref[head] += dot(stack, half, 1, 0)

    @pl.when(step == pl.num_programs(0) - 1)
    def _():
        low, high = where_ref[0], where_ref[1]
        quarter = heads // 4
        for head in range(heads):
            lanes = slice(head * width, (head + 1) * width)
            gain_out_ref[:, lanes] = jnp.sum(gain_total_ref[head], axis=0, keepdims=True)
            piece, inside, place = head // quarter, head % quarter, head % (2 * quarter)
            parts = [
                total_ref[head, level * width : (level + 1) * width, :] * where_ref[level].astype(F32)
                for level in range(depth)
            ]

            @pl.when(low == piece // 2)
            def _():
                mine0_ref[place] = parts[0]
                mine1_ref[place] = parts[1]

            @pl.when(low != piece // 2)
            def _():
                theirs0_ref[place] = parts[0]
                theirs1_ref[place] = parts[1]

            for offset in range(4):
                owner = 2 * other_bit(low, offset & 1) + other_bit(high, offset >> 1)

                @pl.when(owner == piece)
                def _():
                    quarter_refs[offset][inside] = parts[2]

            for level in range(3, depth):
                extra_refs[level - 3][head] = parts[level]


def main_kernel(
    base, where_ref, query_ref, key_ref, value_ref, local_ref, half_ref, coef_ref, wide_ref, *refs
):
    previous, refs = refs[:-7], refs[-7:]
    grad_query_ref, key_sum_ref, value_sum_ref, level_ref, pick_ref, key_acc, value_acc = refs
    levels = coef_ref.shape[0]
    head = base + pl.program_id(0)
    rows, width = query_ref.shape
    tile = min(TILE, rows)

    @pl.when(pl.program_id(0) == 0)
    def _():
        shape = pick_ref.shape
        picked = lax.broadcasted_iota(jnp.int32, shape, 0) // width == lax.broadcasted_iota(
            jnp.int32, shape, 1
        )
        pick_ref[...] = jnp.where(picked, 1.0, 0.0).astype(BF16)
        if previous:
            level_ref[...] = previous[-1][...]

    columns = level_columns(coef_ref, head)
    first_row = coef_ref[0, pl.ds(head, 1), :]
    keep = lax.broadcasted_iota(jnp.int32, (tile, tile), 0) <= lax.broadcasted_iota(
        jnp.int32, (tile, tile), 1
    )
    for start in range(0, rows, tile):
        span = slice(start, start + tile)
        stop = start + tile
        query = query_ref[span, :]
        half = half_ref[span, :]
        grad = half.astype(F32)
        wide_query = query.astype(F32)
        products = [(grad * local_ref[span, :]).astype(BF16)]
        query_sum = None
        for level in range(levels - 1):
            read = dot(half, wide_ref[0, level * width : (level + 1) * width, :], 1, 1)
            products.append((wide_query * read).astype(BF16))
            part = columns[span, level + 1 : level + 2] * read
            query_sum = part if query_sum is None else query_sum + part
        sums = dot(jnp.concatenate(products, axis=1), pick_ref[...], 1, 0).T
        for level in range(levels):
            level_ref[level, pl.ds(head, 1), span] = sums[level : level + 1, :]

        weighted = (columns[span, 0:1] * grad).astype(BF16)
        scores = dot(key_ref[:stop, :], query, 1, 1)
        pair = dot(value_ref[:stop, :], half, 1, 1) * first_row[:, span]
        kept = [jnp.where(keep, scores[start:], 0.0).astype(BF16)]
        pairs = [jnp.where(keep, pair[start:], 0.0).astype(BF16)]
        if start:
            kept = [scores[:start].astype(BF16)] + kept
            pairs = [pair[:start].astype(BF16)] + pairs
        kept = jnp.concatenate(kept, axis=0)
        pairs = jnp.concatenate(pairs, axis=0)
        value_part = dot(kept, weighted, 1, 0)
        key_part = dot(pairs, query, 1, 0)
        if start:
            value_acc[:start, :] += value_part[:start]
            key_acc[:start, :] += key_part[:start]
        value_acc[span, :] = value_part[start:]
        key_acc[span, :] = key_part[start:]
        grad_query_ref[span, :] = (query_sum + dot(pairs, key_ref[:stop, :], 0, 0)).astype(BF16)
    key_sum_ref[...] = key_acc[...]
    value_sum_ref[...] = value_acc[...]


def final_kernel(where_ref, key_ref, value_ref, key_sum_ref, value_sum_ref, own_ref, add_ref, other_ref, *refs):
    extra, (key_out_ref, value_out_ref) = refs[:-2], refs[-2:]
    head = pl.program_id(0)
    half = own_ref.shape[0]
    place = head % half
    mine = head // half == where_ref[0]
    state = jnp.where(mine, own_ref[place] + add_ref[place], other_ref[place])
    if extra:
        state += extra[0][head]
    state = state.astype(BF16)
    key_out_ref[...] = (key_sum_ref[...] + dot(value_ref[...], state, 1, 1)).astype(BF16)
    value_out_ref[...] = (value_sum_ref[...] + dot(key_ref[...], state, 1, 0)).astype(BF16)


def send(block, count, mask, keep=lambda place: True):
    return lax.ppermute(block, "seq", [(g, g ^ mask) for g in range(count) if keep(g)])


def body(count, heads_all, query, key, value, level_coef, gain, cotangent):
    rows = query.shape[0]
    heads = level_coef.shape[1]
    width = query.shape[1] // heads
    depth = level_coef.shape[0] - 1
    features = heads_all * query.shape[1]
    half, quarter = heads // 2, heads // 4
    group = lax.axis_index("seq")
    where = jnp.stack([group // 2**level % 2 for level in range(depth)]).astype(jnp.int32)
    gain_row = gain.reshape(1, -1)
    size = rows * heads * width
    square = size * width

    def spec(shape, at):
        return pl.BlockSpec(shape, at)

    def whole(*shape):
        return pl.BlockSpec(shape, lambda h, where: (0,) * len(shape))

    def shaped(*shape, dtype=F32):
        return jax.ShapeDtypeStruct(shape, dtype)

    def call(kernel, name, grid, flops, moved, in_specs, out_specs, out_shape, scratch=(), aliases=None):
        return pl.pallas_call(
            kernel,
            grid_spec=pltpu.PrefetchScalarGridSpec(
                num_scalar_prefetch=1,
                grid=(grid,),
                in_specs=in_specs,
                out_specs=out_specs,
                scratch_shapes=scratch,
            ),
            out_shape=out_shape,
            name=name,
            input_output_aliases=aliases or {},
            compiler_params=pltpu.CompilerParams(
                dimension_semantics=("arbitrary",), vmem_limit_bytes=VMEM_LIMIT
            ),
            cost_estimate=pl.CostEstimate(flops=flops, bytes_accessed=moved, transcendentals=0),
        )

    def states(mine):
        at = spec(
            (rows, width),
            lambda h, where: (0, h + half * (where[0] if mine else 1 - where[0])),
        )
        return call(
            states_kernel,
            "states",
            half,
            square,
            2 * size,
            [at, at],
            spec((1, width, width), lambda h, where: (h, 0, 0)),
            shaped(half, width, width),
        )(where, key, value)

    def bit(place, level):
        return place >> level & 1

    token = spec((rows, width), lambda h, where: (0, h))
    gain_spec = spec((1, width), lambda h, where: (0, h))
    token_f32 = shaped(rows, heads * width)
    token_bf16 = shaped(rows, heads * width, dtype=BF16)
    coef_spec = whole(*level_coef.shape)
    half_spec = whole(half, width, width)
    quarter_spec = whole(quarter, width, width)
    full_spec = whole(heads, width, width)
    half_f32 = shaped(half, width, width)
    quarter_f32 = shaped(quarter, width, width)
    full_f32 = shaped(heads, width, width)

    theirs = states(False)
    first = send(theirs, count, 1)
    mine = states(True)

    local = call(
        local_kernel,
        "local",
        heads,
        3 * rows * size,
        10 * size,
        [token, token, token],
        token,
        token_f32,
    )(where, query, key, value)

    first_rest = send(mine, count, 1, lambda g: not bit(g, 0))
    pair = mine + first
    second = send(pair, count, 2, lambda g: not bit(g, 1))
    second_rest = send(second, count, 1, lambda g: bit(g, 1))
    four = pair + second
    near = send(four[:quarter], count, 6, lambda g: bit(g, 1) and not bit(g, 2))
    far = send(four[quarter:], count, 4, lambda g: bit(g, 1) and not bit(g, 2))
    third = near + far
    third_rest = [send(third, count, mask, lambda g: bit(g, 2)) for mask in (1, 2, 3)]
    buckets = [first, first_rest, second, second_rest, third] + third_rest
    bucket_specs = [half_spec] * 4 + [quarter_spec] * 4
    if depth > 3:
        low = (where[0] == 0)[None, None, None]
        block = jnp.concatenate([jnp.where(low, mine, theirs), jnp.where(low, theirs, mine)])
        for level in range(3):
            block = block + send(block, count, 1 << level)
        for level in range(3, depth):
            other = send(block, count, 1 << level)
            buckets.append(other)
            bucket_specs.append(full_spec)
            block = block + other

    coef_rows = level_coef.reshape(-1, rows)

    def across(tile):
        return spec((tile, heads * width), lambda h, where: (h, 0))

    def along(count, tile):
        return spec((count, tile), lambda h, where: (0, h))

    tile = min(TILE // 2, rows)
    output, sums, wide = call(
        output_kernel,
        "output",
        rows // tile,
        2 * depth * square,
        12 * size,
        [across(tile)] * 3 + [whole(1, heads * width), along(coef_rows.shape[0], tile)] + bucket_specs,
        [across(tile), along(2, tile), whole(heads, depth * width, width)],
        [token_f32, shaped(2, rows), shaped(heads, depth * width, width, dtype=BF16)],
    )(where, query, local, cotangent, gain_row, coef_rows, *buckets)

    total = lax.psum(sums, "head")

    extra_count = max(depth - 3, 0)
    tile = min(TILE, rows)
    grads = call(
        functools.partial(bucket_kernel, features),
        "buckets",
        rows // tile,
        2 * depth * square,
        10 * size,
        [across(tile)] * 3 + [whole(1, heads * width), along(coef_rows.shape[0], tile), along(2, tile)],
        [across(tile)] * 2
        + [whole(1, heads * width)]
        + [half_spec] * 4
        + [quarter_spec] * 4
        + [full_spec] * extra_count,
        [token_bf16, token_bf16, shaped(1, heads * width)]
        + [half_f32] * 4
        + [quarter_f32] * 4
        + [full_f32] * extra_count,
        [pltpu.VMEM((heads, depth * width, width), F32), pltpu.VMEM((heads, 8, width), F32)],
    )(where, query, output, cotangent, gain_row, coef_rows, total)
    mixed, grad_half, gain_part, mine0, theirs0, mine1, theirs1 = grads[:7]
    quarters, extra = grads[7:11], grads[11:]

    def main(piece, previous):
        base = piece * quarter
        at = spec((rows, width), lambda h, where: (0, base + h))
        ins = [at] * 5 + [
            coef_spec,
            spec((1, depth * width, width), lambda h, where: (base + h, 0, 0)),
        ]
        aliases = {}
        if previous:
            aliases = {1 + len(ins) + index: index for index in range(3)}
            ins += [pl.BlockSpec(memory_space=pl.ANY)] * 3 + [coef_spec]
        return call(
            functools.partial(main_kernel, base),
            "main",
            quarter,
            (8 * rows * size + 4 * depth * square) // 4,
            22 * size // 4,
            ins,
            [at, at, at, coef_spec],
            [token_bf16, token_f32, token_f32, shaped(*level_coef.shape)],
            [pltpu.VMEM(((depth + 1) * width, width), BF16)] + [pltpu.VMEM((rows, width), F32)] * 2,
            aliases,
        )(where, query, key, value, local, grad_half, level_coef, wide, *previous)

    swapped = send(theirs1, count, 1, lambda g: bit(g, 1))
    gathered = quarters[0]
    for mask in (1, 2, 3):
        gathered = gathered + send(quarters[mask], count, mask, lambda g: bit(g, 2))
    near = send(gathered, count, 6, lambda g: bit(g, 2) and not bit(g, 1))
    far = send(gathered, count, 4, lambda g: bit(g, 2) and bit(g, 1))
    four = jnp.concatenate([near, far])
    down = send(four + mine1 + swapped, count, 2, lambda g: bit(g, 1))
    add = send(theirs0, count, 1, lambda g: bit(g, 0))
    own = four + down
    other = send(own + mine0, count, 1)

    grad_gain = gain_part.reshape(-1)
    for level in range(depth):
        grad_gain = grad_gain + send(grad_gain, count, 1 << level)

    carried = []
    if depth > 3:
        block = send(extra[-1], count, 1 << (depth - 1))
        for level in reversed(range(3, depth - 1)):
            block = block + send(extra[level - 3] + block, count, 1 << level)
        for level in reversed(range(3)):
            block = block + send(block, count, 1 << level)
        carried = [block]

    results = []
    for piece in range(4):
        results = main(piece, results)
    grad_query, key_sum, value_sum, grad_level = results

    grad_key, grad_value = call(
        final_kernel,
        "final",
        heads,
        4 * square,
        16 * size,
        [token, token, token, token] + [half_spec] * 3 + [full_spec] * len(carried),
        [token, token],
        [token_bf16, token_bf16],
    )(where, key, value, key_sum, value_sum, own, add, other, *carried)
    return (mixed, grad_query, grad_key, grad_value, grad_level, grad_gain)


def solution(mesh):
    placed = (
        P("seq", "head"),
        P("seq", "head"),
        P("seq", "head"),
        P(None, "head", "seq"),
        P("head"),
        P("seq", "head"),
    )
    return jax.shard_map(
        functools.partial(body, mesh.shape["seq"], mesh.shape["head"]),
        mesh=mesh,
        in_specs=placed,
        out_specs=(
            P("seq", "head"),
            P("seq", "head"),
            P("seq", "head"),
            P("seq", "head"),
            P(None, "head", "seq"),
            P("head"),
        ),
        check_vma=False,
    )
```

time: 246 us -> 152 us (0.62)
  matrix products: 90.1 us -> 0 us
  Pallas kernels: 0 us -> 68.5 us
  starting transfers between devices: 13.7 us -> 55.5 us
  waiting for transfers between devices: 41.6 us -> 8.73 us
  local copies, waits for them, and re-layouts: 38.8 us -> 10.7 us
  blocking collectives: 32.7 us -> 5.73 us
  other arithmetic: 27.4 us -> 0.88 us
    dot_general x12 -> x0, matrix products: 90.1 us -> none  [the longest x1 12.1 us: body(): jnp.einsum('hts,she->the', kept, v_three, preferred_element_type=f32)]
    pallas_call x0 -> x10, Pallas kernels: none -> 68.5 us  [the longest x4 31.6 us: main(): call(functools.partial(main_kernel, base), 'main', quarter, (8 * rows * s...]
    ppermute x6 -> x21, starting transfers between devices: 13.7 us -> 55.5 us  [send(): lax.ppermute(block, 'seq', [(g, g ^ mask) for g in range(count) if keep(g)])]
    ppermute x6 -> x21, waiting for transfers between devices: 41.6 us -> 8.73 us  [send(): lax.ppermute(block, 'seq', [(g, g ^ mask) for g in range(count) if keep(g)])]
    psum x3 -> x1, blocking collectives: 32.7 us -> 5.73 us  [body(): total = lax.psum(sums, 'head')]
    reduce_sum x3 -> x0, other arithmetic: 16.7 us -> none  [the longest x1 6.69 us: body(): grad_first = jnp.sum(grad_float * local, axis=-1)]
    unnamed x41 -> x29, local copies, waits for them, and re-layouts: 26.4 us -> 10.6 us
    reshape x2 -> x0, local copies, waits for them, and re-layouts: 8.19 us -> none  [the longest x1 4.1 us: body(): k_three = key.reshape(rows, heads_here, width)]
  transfers between devices with their start and end apart: 6 -> 21, of which waited for: 5 -> 2; matrix products, arithmetic and copies ran while one was open for 30% -> 0% of each run, Pallas kernels for 0% -> 29%
where the time goes in v2:
time: 152 us; the launch traced here: 151 us
  Pallas kernels  68.5 us (45%)
  starting transfers between devices  55.5 us (37%)
  local copies, waits for them, and re-layouts  10.7 us (7%)
  waiting for transfers between devices  8.73 us (6%)
  blocking collectives  5.73 us (4%)
    ppermute x21, starting transfers between devices, send(): lax.ppermute(block, 'seq', [(g, g ^ mask) for g in range(count) if keep(g)])  55.5 us
    pallas_call x4, Pallas kernels, main(): call(functools.partial(main_kernel, base), 'main', quarter, (8 * rows * s...  31.6 us
    unnamed x29, local copies, waits for them, and re-layouts  10.6 us
    pallas_call x1, Pallas kernels, body(): call(local_kernel, 'local', heads, 3 * rows * size, 10 * size, [token, to...  10.2 us
    pallas_call x1, Pallas kernels, body(): call(output_kernel, 'output', rows // tile, 2 * depth * square, 12 * size...  8.83 us
    ppermute x21, waiting for transfers between devices, send(): lax.ppermute(block, 'seq', [(g, g ^ mask) for g in range(count) if keep(g)])  8.73 us
    pallas_call x1, Pallas kernels, body(): call(final_kernel, 'final', heads, 4 * square, 16 * size, [token, token,...  6.74 us
    pallas_call x1, Pallas kernels, body(): call(functools.partial(bucket_kernel, features), 'buckets', rows // tile,...  6.52 us
  transfers between devices with their start and end apart: 21, of which 2 were waited for; matrix products, arithmetic and copies ran while one was open for 0% of the time, Pallas kernels for 29%

profile of v2, /device:TPU:0, one launch (start us, length us, event | category | flops | bytes accessed | tf_op | source)
XLA Modules:
  0.0 151.1 jit_solution(8738441230798125843)
XLA Ops:
  0.8 1.6 %copy-done.2 = bf16[1024,1024]{1,0:T(8,128)(2,1)S(1)} copy-done((bf16[1024,1024]{1,0:T(8,128)(2,1)S(1)}, bf16[1024,1024]{1,0:T(8,128)(2,1)}, u32[]{:S(2)}) %copy-start.2) | copy-done | bytes 2097176
  2.4 1.6 %copy-done.4 = bf16[1024,1024]{1,0:T(8,128)(2,1)S(1)} copy-done((bf16[1024,1024]{1,0:T(8,128)(2,1)S(1)}, bf16[1024,1024]{1,0:T(8,128)(2,1)}, u32[]{:S(2)}) %copy-start.4) | copy-done | bytes 2097176
  3.9 2.3 %states.2 = f32[4,128,128]{2,1,0:T(8,128)S(1)} custom-call(s32[3]{0:T(128)S(1)} %pad_add_fusion.where_ref, bf16[1024,1024]{1,0:T(8,128)(2,1)S(1)} %copy-done.2, bf16[1024,1024]{1,0:T(8,128)(2,1)S(1)} %copy-done.4), custom_call_target="tpu_custom_call" | custom-call | flops 134217728 | bytes 2097152 | tf_op jit(solution)/shard_map/states/pallas_call | solution.py:308
  6.2 3.1 %collective-permute-start = (f32[4,128,128]{2,1,0:T(8,128)S(1)}, f32[4,128,128]{2,1,0:T(8,128)S(1)}, u32[]{:S(2)}, u32[]{:S(2)}) collective-permute-start(f32[4,128,128]{2,1,0:T(8,128)S(1)} %states.2), channel_id=1, source_target_pairs={{0,4},{4,0},{8,12},{12,8},{16,20},{20,16},{24,28},{28,24},{1,5},{5... | collective-permute-start | bytes 786440 | tf_op jit(solution)/shard_map/ppermute | solution.py:259
  9.3 2.3 %states.3 = f32[4,128,128]{2,1,0:T(8,128)S(1)} custom-call(s32[3]{0:T(128)S(1)} %pad_add_fusion.where_ref, bf16[1024,1024]{1,0:T(8,128)(2,1)S(1)} %copy-done.2, bf16[1024,1024]{1,0:T(8,128)(2,1)S(1)} %copy-done.4), custom_call_target="tpu_custom_call" | custom-call | flops 134217728 | bytes 2097152 | tf_op jit(solution)/shard_map/states/pallas_call | solution.py:308
  11.6 4.0 %collective-permute-done.refs_0_ = f32[4,128,128]{2,1,0:T(8,128)S(1)} collective-permute-done((f32[4,128,128]{2,1,0:T(8,128)S(1)}, f32[4,128,128]{2,1,0:T(8,128)S(1)}, u32[]{:S(2)}, u32[]{:S(2)}) %collective-permute-start) | collective-permute-done | bytes 262176 | tf_op jit(solution)/shard_map/ppermute | solution.py:259
  15.6 3.7 %collective-permute-start.2 = (f32[4,128,128]{2,1,0:T(8,128)S(1)}, f32[4,128,128]{2,1,0:T(8,128)S(1)}, u32[]{:S(2)}, u32[]{:S(2)}) collective-permute-start(f32[4,128,128]{2,1,0:T(8,128)S(1)} %add.57), channel_id=1, source_target_pairs={{0,8},{4,12},{16,24},{20,28},{1,9},{5,13},{17,25},{21,29},{2,10},{... | collective-permute-start | bytes 786440 | tf_op jit(solution)/shard_map/ppermute | solution.py:259
  19.4 4.7 %collective-permute-done.2.refs_2_ = f32[4,128,128]{2,1,0:T(8,128)S(1)} collective-permute-done((f32[4,128,128]{2,1,0:T(8,128)S(1)}, f32[4,128,128]{2,1,0:T(8,128)S(1)}, u32[]{:S(2)}, u32[]{:S(2)}) %collective-permute-start.2) | collective-permute-done | bytes 262176 | tf_op jit(solution)/shard_map/ppermute | solution.py:259
  24.1 0.7 collective-permute-start.5
  25.5 3.4 %collective-permute-start.1 = (f32[4,128,128]{2,1,0:T(8,128)S(1)}, f32[4,128,128]{2,1,0:T(8,128)S(1)}, u32[]{:S(2)}, u32[]{:S(2)}) collective-permute-start(f32[4,128,128]{2,1,0:T(8,128)S(1)} %states.3), channel_id=1, source_target_pairs={{0,4},{8,12},{16,20},{24,28},{1,5},{9,13},{17,21},{25,29},{2,6},{1... | collective-permute-start | bytes 786440 | tf_op jit(solution)/shard_map/ppermute | solution.py:259
  28.9 0.7 collective-permute-start.3
  29.7 0.8 collective-permute-start.8
  31.8 10.2 %local.1.local_ref = f32[1024,1024]{1,0:T(8,128)S(1)} custom-call(s32[3]{0:T(128)S(1)} %pad_add_fusion.where_ref, bf16[1024,1024]{1,0:T(8,128)(2,1)S(1)} %copy-done.6, bf16[1024,1024]{1,0:T(8,128)(2,1)S(1)} %copy-done.3, bf16[1024,1024]{1,0:T(8,128)(2,1)S(1)} %copy-done.4), custom_call_target="tpu_custom_call" | custom-call | flops 3221225472 | bytes 10485760 | tf_op jit(solution)/shard_map/local/pallas_call | solution.py:338
  42.2 8.8 %output.1 = (f32[1024,1024]{1,0:T(8,128)S(1)}, f32[2,1024]{1,0:T(2,128)S(1)}, bf16[8,384,128]{2,1,0:T(8,128)(2,1)S(1)}) custom-call(s32[3]{0:T(128)S(1)} %pad_add_fusion.where_ref, bf16[1024,1024]{1,0:T(8,128)(2,1)S(1)} %copy-done.6, f32[1024,1024]{1,0:T(8,128)S(1)} %local.1.local_ref, bf16[1024,1024]{1,0:T(8,128)(2,1)S(1)} %copy-done.8, ...), custom_call_target="tpu_custom_call" | custom-call | flops 805306368 | bytes 12582912 | tf_op jit(solution)/shard_map/output/pallas_call | solution.py:380
  51.0 2.0 %copy-done.11 = f32[1024,1024]{1,0:T(8,128)} copy-done((f32[1024,1024]{1,0:T(8,128)}, f32[1024,1024]{1,0:T(8,128)S(1)}, u32[]{:S(2)}) %copy-start.11) | copy-done | bytes 4194328
  53.1 5.7 %psum.7.sums_ref = f32[2,1024]{1,0:T(2,128)S(1)} all-reduce(f32[2,1024]{1,0:T(2,128)S(1)} %get-tuple-element.39), channel_id=1, replica_groups=mesh['seq'=8,'head'=4] {'head'}, use_global_device_ids=true, to_apply=%region_0.1 | all-reduce | flops 2048 | bytes 16384 | tf_op jit(solution)/shard_map/psum | solution.py:391
  58.8 1.6 %copy-done.7 = bf16[1024,1024]{1,0:T(8,128)(2,1)S(1)} copy-done((bf16[1024,1024]{1,0:T(8,128)(2,1)S(1)}, bf16[1024,1024]{1,0:T(8,128)(2,1)}, u32[]{:S(2)}) %copy-start.7) | copy-done | bytes 2097176
  60.4 1.6 %copy-done.9 = bf16[1024,1024]{1,0:T(8,128)(2,1)S(1)} copy-done((bf16[1024,1024]{1,0:T(8,128)(2,1)S(1)}, bf16[1024,1024]{1,0:T(8,128)(2,1)}, u32[]{:S(2)}) %copy-start.9) | copy-done | bytes 2097176
  62.0 2.2 %copy-done.12 = f32[1024,1024]{1,0:T(8,128)S(1)} copy-done((f32[1024,1024]{1,0:T(8,128)S(1)}, f32[1024,1024]{1,0:T(8,128)}, u32[]{:S(2)}) %copy-start.12) | copy-done | bytes 4194328
  64.2 6.5 %buckets.1 = (bf16[1024,1024]{1,0:T(8,128)(2,1)}, bf16[1024,1024]{1,0:T(8,128)(2,1)S(1)}, f32[1,1024]{1,0:T(1,128)S(1)}, f32[4,128,128]{2,1,0:T(8,128)S(1)}, f32...) custom-call(s32[3]{0:T(128)S(1)} %pad_add_fusion.where_ref, ...), custom_call_target="tpu_custom_call" | custom-call | flops 805306368 | bytes 10485760 | tf_op jit(solution)/shard_map/buckets/pallas_call | solution.py:395
  70.7 0.8 collective-permute-start.9
  73.6 0.7 collective-permute-start.14
  75.0 1.3 collective-permute-start.16
  76.5 1.5 collective-permute-start.15
  78.0 7.8 %main.4 = (bf16[1024,1024]{1,0:T(8,128)(2,1)}, f32[1024,1024]{1,0:T(8,128)S(1)}, f32[1024,1024]{1,0:T(8,128)S(1)}, f32[4,8,1024]{2,1,0:T(8,128)S(1)}) custom-call(s32[3]{0:T(128)S(1)} %pad_add_fusion.where_ref, bf16[1024,1024]{1,0:T(8,128)(2,1)S(1)} %copy-done.7, bf16[1024,1024]{1,0:T(8,128)(2,1)S(1)} %copy-done.3, bf16[1024,1024]{1,0:T(8,128)(2,1)S(1)} %copy-done.5, ...), custom_call_target="tpu_custom_call" | custom-call | flops 2550136832 | bytes 5767168 | tf_op jit(solution)/shard_map/main/pallas_call | solution.py:427
  85.8 7.8 %main.5 = (bf16[1024,1024]{1,0:T(8,128)(2,1)}, f32[1024,1024]{1,0:T(8,128)S(1)}, f32[1024,1024]{1,0:T(8,128)S(1)}, f32[4,8,1024]{2,1,0:T(8,128)S(1)}) custom-call(s32[3]{0:T(128)S(1)} %pad_add_fusion.where_ref, bf16[1024,1024]{1,0:T(8,128)(2,1)S(1)} %copy-done.7, ...), custom_call_target="tpu_custom_call", output_to_operand_aliasing={{0}: (8, {}), {1}: (9, {}), {2}: (10, {})} | custom-call | flops 2550136832 | bytes 5767168 | tf_op jit(solution)/shard_map/main/pallas_call | solution.py:427
  93.6 31.4 %collective-permute-start.19 = (f32[1024]{0:T(1024)S(1)}, f32[1024]{0:T(1024)S(1)}, u32[]{:S(2)}, u32[]{:S(2)}) collective-permute-start(f32[1024]{0:T(1024)S(1)} %add.67), channel_id=1, source_target_pairs={{0,8},{4,12},{8,0},{12,4},{16,24},{20,28},{24,16},{28,20},{1,9},{5... | collective-permute-start | bytes 12296 | tf_op jit(solution)/shard_map/ppermute | solution.py:259
  125.1 1.6 %collective-permute-start.17 = (f32[4,128,128]{2,1,0:T(8,128)S(1)}, f32[4,128,128]{2,1,0:T(8,128)S(1)}, u32[]{:S(2)}, u32[]{:S(2)}) collective-permute-start(f32[4,128,128]{2,1,0:T(8,128)S(1)} %get-tuple-element.70), channel_id=1, source_target_pairs={{0,4},{4,0},{8,12},{12,8},{16,20},{20,16},{24,28},{28,24},{1,5},{5... | collective-permute-start | bytes 786440 | tf_op jit(solution)/shard_map/ppermute | solution.py:259
  126.7 7.8 %main.6 = (bf16[1024,1024]{1,0:T(8,128)(2,1)}, f32[1024,1024]{1,0:T(8,128)S(1)}, f32[1024,1024]{1,0:T(8,128)S(1)}, f32[4,8,1024]{2,1,0:T(8,128)S(1)}) custom-call(s32[3]{0:T(128)S(1)} %pad_add_fusion.where_ref, bf16[1024,1024]{1,0:T(8,128)(2,1)S(1)} %copy-done.7, ...), custom_call_target="tpu_custom_call", output_to_operand_aliasing={{0}: (8, {}), {1}: (9, {}), {2}: (10, {})} | custom-call | flops 2550136832 | bytes 5767168 | tf_op jit(solution)/shard_map/main/pallas_call | solution.py:427
  134.5 1.1 collective-permute-start.20
  135.6 8.1 %main.7 = (bf16[1024,1024]{1,0:T(8,128)(2,1)}, f32[1024,1024]{1,0:T(8,128)S(1)}, f32[1024,1024]{1,0:T(8,128)S(1)}, f32[4,8,1024]{2,1,0:T(8,128)}) custom-call(s32[3]{0:T(128)S(1)} %pad_add_fusion.where_ref, bf16[1024,1024]{1,0:T(8,128)(2,1)S(1)} %copy-done.7, ...), custom_call_target="tpu_custom_call", output_to_operand_aliasing={{0}: (8, {}), {1}: (9, {}), {2}: (10, {})} | custom-call | flops 2550136832 | bytes 5767168 | tf_op jit(solution)/shard_map/main/pallas_call | solution.py:427
  144.4 6.7 %final.1 = (bf16[1024,1024]{1,0:T(8,128)(2,1)}, bf16[1024,1024]{1,0:T(8,128)(2,1)}) custom-call(s32[3]{0:T(128)S(1)} %pad_add_fusion.where_ref, bf16[1024,1024]{1,0:T(8,128)(2,1)S(1)} %copy-done.3, bf16[1024,1024]{1,0:T(8,128)(2,1)S(1)} %copy-done.5, f32[1024,1024]{1,0:T(8,128)S(1)} %get-tuple-element.56.key_sum_ref, ...), custom_call_target="tpu_custom_call" | custom-call | flops 536870912 | bytes 16777216 | tf_op jit(solution)/shard_map/final/pallas_call | solution.py:470
  (62 shorter events, 5.8 us)
Async XLA Ops:
  6.2 9.4 %collective-permute-start = (f32[4,128,128]{2,1,0:T(8,128)S(1)}, f32[4,128,128]{2,1,0:T(8,128)S(1)}, u32[]{:S(2)}, u32[]{:S(2)}) collective-permute-start(f32[4,128,128]{2,1,0:T(8,128)S(1)} %states.2), channel_id=1, source_target_pairs={{0,4},{4,0},{8,12},{12,8},{16,20},{20,16},{24,28},{28,24},{1,5},{5... | collective-permute-start | bytes 786440 | tf_op jit(solution)/shard_map/ppermute | solution.py:259
  9.3 22.5 %copy-start.6 = (bf16[1024,1024]{1,0:T(8,128)(2,1)S(1)}, bf16[1024,1024]{1,0:T(8,128)(2,1)}, u32[]{:S(2)}) copy-start(bf16[1024,1024]{1,0:T(8,128)(2,1)} %query_ref.13) | copy-start | bytes 6291460
  11.6 20.2 %copy-start.3 = (bf16[1024,1024]{1,0:T(8,128)(2,1)S(1)}, bf16[1024,1024]{1,0:T(8,128)(2,1)}, u32[]{:S(2)}) copy-start(bf16[1024,1024]{1,0:T(8,128)(2,1)} %key_ref.15) | copy-start | bytes 6291460
  15.6 8.4 %collective-permute-start.2 = (f32[4,128,128]{2,1,0:T(8,128)S(1)}, f32[4,128,128]{2,1,0:T(8,128)S(1)}, u32[]{:S(2)}, u32[]{:S(2)}) collective-permute-start(f32[4,128,128]{2,1,0:T(8,128)S(1)} %add.57), channel_id=1, source_target_pairs={{0,8},{4,12},{16,24},{20,28},{1,9},{5,13},{17,25},{21,29},{2,10},{... | collective-permute-start | bytes 786440 | tf_op jit(solution)/shard_map/ppermute | solution.py:259
  24.1 5.5 %collective-permute-start.5 = (f32[2,128,128]{2,1,0:T(8,128)S(1)}, f32[2,128,128]{2,1,0:T(8,128)S(1)}, u32[]{:S(2)}, u32[]{:S(2)}) collective-permute-start(f32[2,128,128]{2,1,0:T(8,128)S(1)} %get-tuple-element.72), channel_id=1, source_target_pairs={{8,24},{12,28},{9,25},{13,29},{10,26},{14,30},{11,27},{15,31}} | collective-permute-start | bytes 393224 | tf_op jit(solution)/shard_map/ppermute | solution.py:259
  24.8 4.8 %collective-permute-start.4 = (f32[2,128,128]{2,1,0:T(8,128)S(1)}, f32[2,128,128]{2,1,0:T(8,128)S(1)}, u32[]{:S(2)}, u32[]{:S(2)}) collective-permute-start(f32[2,128,128]{2,1,0:T(8,128)S(1)} %get-tuple-element.73), channel_id=1, source_target_pairs={{8,16},{12,20},{9,17},{13,21},{10,18},{14,22},{11,19},{15,23}} | collective-permute-start | bytes 393224 | tf_op jit(solution)/shard_map/ppermute | solution.py:259
  25.5 16.6 %collective-permute-start.1 = (f32[4,128,128]{2,1,0:T(8,128)S(1)}, f32[4,128,128]{2,1,0:T(8,128)S(1)}, u32[]{:S(2)}, u32[]{:S(2)}) collective-permute-start(f32[4,128,128]{2,1,0:T(8,128)S(1)} %states.3), channel_id=1, source_target_pairs={{0,4},{8,12},{16,20},{24,28},{1,5},{9,13},{17,21},{25,29},{2,6},{1... | collective-permute-start | bytes 786440 | tf_op jit(solution)/shard_map/ppermute | solution.py:259
  28.9 13.2 %collective-permute-start.3 = (f32[4,128,128]{2,1,0:T(8,128)S(1)}, f32[4,128,128]{2,1,0:T(8,128)S(1)}, u32[]{:S(2)}, u32[]{:S(2)}) collective-permute-start(f32[4,128,128]{2,1,0:T(8,128)S(1)} %collective-permute-done.2.refs_2_), channel_id=1, source_target_pairs={{8,12},{12,8},{24,28},{28,24},{9,13},{13,9},{25,29},{29,25},{10,14... | collective-permute-start | bytes 786440 | tf_op jit(solution)/shard_map/ppermute | solution.py:259
  29.6 12.5 %copy-start.8 = (bf16[1024,1024]{1,0:T(8,128)(2,1)S(1)}, bf16[1024,1024]{1,0:T(8,128)(2,1)}, u32[]{:S(2)}) copy-start(bf16[1024,1024]{1,0:T(8,128)(2,1)} %cot_ref.3) | copy-start | bytes 6291460
  29.6 12.5 %copy-start.10 = (f32[4,8,1024]{2,1,0:T(8,128)S(1)}, f32[4,8,1024]{2,1,0:T(8,128)}, u32[]{:S(2)}) copy-start(f32[4,8,1024]{2,1,0:T(8,128)} %coef_ref.7) | copy-start | bytes 393220
  29.7 12.5 %copy-start.13 = (f32[1024]{0:T(1024)S(1)}, f32[1024]{0:T(1024)}, u32[]{:S(2)}) copy-start(f32[1024]{0:T(1024)} %param.10) | copy-start | bytes 12292
  29.7 12.5 %collective-permute-start.8 = (f32[2,128,128]{2,1,0:T(8,128)S(1)}, f32[2,128,128]{2,1,0:T(8,128)S(1)}, u32[]{:S(2)}, u32[]{:S(2)}) collective-permute-start(f32[2,128,128]{2,1,0:T(8,128)S(1)} %add.59.refs_4_), channel_id=1, source_target_pairs={{16,28},{20,24},{24,20},{28,16},{17,29},{21,25},{25,21},{29,17},{1... | collective-permute-start | bytes 393224 | tf_op jit(solution)/shard_map/ppermute | solution.py:259
  30.5 11.7 %collective-permute-start.7 = (f32[2,128,128]{2,1,0:T(8,128)S(1)}, f32[2,128,128]{2,1,0:T(8,128)S(1)}, u32[]{:S(2)}, u32[]{:S(2)}) collective-permute-start(f32[2,128,128]{2,1,0:T(8,128)S(1)} %add.59.refs_4_), channel_id=1, source_target_pairs={{16,24},{20,28},{24,16},{28,20},{17,25},{21,29},{25,17},{29,21},{1... | collective-permute-start | bytes 393224 | tf_op jit(solution)/shard_map/ppermute | solution.py:259
  31.1 11.0 %collective-permute-start.6 = (f32[2,128,128]{2,1,0:T(8,128)S(1)}, f32[2,128,128]{2,1,0:T(8,128)S(1)}, u32[]{:S(2)}, u32[]{:S(2)}) collective-permute-start(f32[2,128,128]{2,1,0:T(8,128)S(1)} %add.59.refs_4_), channel_id=1, source_target_pairs={{16,20},{20,16},{24,28},{28,24},{17,21},{21,17},{25,29},{29,25},{1... | collective-permute-start | bytes 393224 | tf_op jit(solution)/shard_map/ppermute | solution.py:259
  42.1 8.9 %copy-start = (f32[1024,1024]{1,0:T(8,128)}, f32[1024,1024]{1,0:T(8,128)S(1)}, u32[]{:S(2)}) copy-start(f32[1024,1024]{1,0:T(8,128)S(1)} %local.1.local_ref) | copy-start | bytes 12582916
  51.0 2.1 %copy-start.11 = (f32[1024,1024]{1,0:T(8,128)}, f32[1024,1024]{1,0:T(8,128)S(1)}, u32[]{:S(2)}) copy-start(f32[1024,1024]{1,0:T(8,128)S(1)} %get-tuple-element.38.out_ref) | copy-start | bytes 12582916
  58.8 1.6 %copy-start.7 = (bf16[1024,1024]{1,0:T(8,128)(2,1)S(1)}, bf16[1024,1024]{1,0:T(8,128)(2,1)}, u32[]{:S(2)}) copy-start(bf16[1024,1024]{1,0:T(8,128)(2,1)} %query_ref.13) | copy-start | bytes 6291460
  62.0 2.2 %copy-start.12 = (f32[1024,1024]{1,0:T(8,128)S(1)}, f32[1024,1024]{1,0:T(8,128)}, u32[]{:S(2)}) copy-start(f32[1024,1024]{1,0:T(8,128)} %copy-done.11) | copy-start | bytes 12582916
  64.2 13.8 %copy-start.1 = (f32[1024,1024]{1,0:T(8,128)S(1)}, f32[1024,1024]{1,0:T(8,128)}, u32[]{:S(2)}) copy-start(f32[1024,1024]{1,0:T(8,128)} %copy-done) | copy-start | bytes 12582916
  70.7 7.3 %copy-start.5 = (bf16[1024,1024]{1,0:T(8,128)(2,1)S(1)}, bf16[1024,1024]{1,0:T(8,128)(2,1)}, u32[]{:S(2)}) copy-start(bf16[1024,1024]{1,0:T(8,128)(2,1)} %value_ref.15) | copy-start | bytes 6291460
  70.7 2.2 %collective-permute-start.9 = (f32[2,128,128]{2,1,0:T(8,128)S(1)}, f32[2,128,128]{2,1,0:T(8,128)S(1)}, u32[]{:S(2)}, u32[]{:S(2)}) collective-permute-start(f32[2,128,128]{2,1,0:T(8,128)S(1)} %get-tuple-element.59), channel_id=1, source_target_pairs={{16,20},{20,16},{24,28},{28,24},{17,21},{21,17},{25,29},{29,25},{1... | collective-permute-start | bytes 393224 | tf_op jit(solution)/shard_map/ppermute | solution.py:259
  71.5 1.4 collective-permute-start.10
  72.2 0.7 collective-permute-start.11
  72.9 3.4 %collective-permute-start.12 = (f32[2,128,128]{2,1,0:T(8,128)S(1)}, f32[2,128,128]{2,1,0:T(8,128)S(1)}, u32[]{:S(2)}, u32[]{:S(2)}) collective-permute-start(f32[2,128,128]{2,1,0:T(8,128)S(1)} %add_add_fusion.1), channel_id=1, source_target_pairs={{16,8},{20,12},{17,9},{21,13},{18,10},{22,14},{19,11},{23,15}} | collective-permute-start | bytes 393224 | tf_op jit(solution)/shard_map/ppermute | solution.py:259
  73.6 2.8 %collective-permute-start.14 = (f32[4,128,128]{2,1,0:T(8,128)S(1)}, f32[4,128,128]{2,1,0:T(8,128)S(1)}, u32[]{:S(2)}, u32[]{:S(2)}) collective-permute-start(f32[4,128,128]{2,1,0:T(8,128)S(1)} %get-tuple-element.63), channel_id=1, source_target_pairs={{8,12},{12,8},{24,28},{28,24},{9,13},{13,9},{25,29},{29,25},{10,14... | collective-permute-start | bytes 786440 | tf_op jit(solution)/shard_map/ppermute | solution.py:259
  74.3 2.1 %collective-permute-start.13 = (f32[2,128,128]{2,1,0:T(8,128)S(1)}, f32[2,128,128]{2,1,0:T(8,128)S(1)}, u32[]{:S(2)}, u32[]{:S(2)}) collective-permute-start(f32[2,128,128]{2,1,0:T(8,128)S(1)} %add_add_fusion.1), channel_id=1, source_target_pairs={{24,8},{28,12},{25,9},{29,13},{26,10},{30,14},{27,11},{31,15}} | collective-permute-start | bytes 393224 | tf_op jit(solution)/shard_map/ppermute | solution.py:259
  75.0 18.6 %collective-permute-start.18 = (f32[1024]{0:T(1024)S(1)}, f32[1024]{0:T(1024)S(1)}, u32[]{:S(2)}, u32[]{:S(2)}) collective-permute-start(f32[1024]{0:T(1024)S(1)} %bitcast.10), channel_id=1, source_target_pairs={{0,4},{4,0},{8,12},{12,8},{16,20},{20,16},{24,28},{28,24},{1,5},{5... | collective-permute-start | bytes 12296 | tf_op jit(solution)/shard_map/ppermute | solution.py:259
  75.0 69.3 %collective-permute-start.16 = (f32[4,128,128]{2,1,0:T(8,128)S(1)}, f32[4,128,128]{2,1,0:T(8,128)S(1)}, u32[]{:S(2)}, u32[]{:S(2)}) collective-permute-start(f32[4,128,128]{2,1,0:T(8,128)S(1)} %get-tuple-element.64), channel_id=1, source_target_pairs={{4,0},{12,8},{20,16},{28,24},{5,1},{13,9},{21,17},{29,25},{6,2},{1... | collective-permute-start | bytes 786440 | tf_op jit(solution)/shard_map/ppermute | solution.py:259
  76.5 48.6 %collective-permute-start.15 = (f32[4,128,128]{2,1,0:T(8,128)S(1)}, f32[4,128,128]{2,1,0:T(8,128)S(1)}, u32[]{:S(2)}, u32[]{:S(2)}) collective-permute-start(f32[4,128,128]{2,1,0:T(8,128)S(1)} %add_add_fusion), channel_id=1, source_target_pairs={{8,0},{12,4},{24,16},{28,20},{9,1},{13,5},{25,17},{29,21},{10,2},{... | collective-permute-start | bytes 786440 | tf_op jit(solution)/shard_map/ppermute | solution.py:259
  93.6 40.9 %collective-permute-start.19 = (f32[1024]{0:T(1024)S(1)}, f32[1024]{0:T(1024)S(1)}, u32[]{:S(2)}, u32[]{:S(2)}) collective-permute-start(f32[1024]{0:T(1024)S(1)} %add.67), channel_id=1, source_target_pairs={{0,8},{4,12},{8,0},{12,4},{16,24},{20,28},{24,16},{28,20},{1,9},{5... | collective-permute-start | bytes 12296 | tf_op jit(solution)/shard_map/ppermute | solution.py:259
  125.1 19.3 %collective-permute-start.17 = (f32[4,128,128]{2,1,0:T(8,128)S(1)}, f32[4,128,128]{2,1,0:T(8,128)S(1)}, u32[]{:S(2)}, u32[]{:S(2)}) collective-permute-start(f32[4,128,128]{2,1,0:T(8,128)S(1)} %get-tuple-element.70), channel_id=1, source_target_pairs={{0,4},{4,0},{8,12},{12,8},{16,20},{20,16},{24,28},{28,24},{1,5},{5... | collective-permute-start | bytes 786440 | tf_op jit(solution)/shard_map/ppermute | solution.py:259
  134.5 9.3 %collective-permute-start.20 = (f32[1024]{0:T(1024)S(1)}, f32[1024]{0:T(1024)S(1)}, u32[]{:S(2)}, u32[]{:S(2)}) collective-permute-start(f32[1024]{0:T(1024)S(1)} %add.68), channel_id=1, source_target_pairs={{0,16},{4,20},{8,24},{12,28},{16,0},{20,4},{24,8},{28,12},{1,17},{... | collective-permute-start | bytes 12296 | tf_op jit(solution)/shard_map/ppermute | solution.py:259
  (3 other events, 4.8 us)

commit v3 on v2

--- a/solution.py
+++ b/solution.py
@@ -37,19 +37,21 @@
     out_ref[0] = dot(key_ref[...], value_ref[...], 0, 0)
 
 
-def local_kernel(where_ref, query_ref, key_ref, value_ref, out_ref):
-    rows = query_ref.shape[0]
+def local_kernel(base, where_ref, query_ref, key_ref, value_ref, *refs):
+    out_ref = refs[-1]
+    rows, width = out_ref.shape
+    lanes = pl.ds(pl.multiple_of((base + pl.program_id(0)) * width, width), width)
     tile = min(TILE, rows)
     keep = lax.broadcasted_iota(jnp.int32, (tile, tile), 0) >= lax.broadcasted_iota(
         jnp.int32, (tile, tile), 1
     )
     for start in range(0, rows, tile):
         span = slice(start, start + tile)
-        scores = dot(query_ref[start:, :], key_ref[span, :], 1, 1)
+        scores = dot(query_ref[start:, lanes], key_ref[span, lanes], 1, 1)
         kept = [jnp.where(keep, scores[:tile], 0.0).astype(BF16)]
         if start + tile < rows:
             kept.append(scores[tile:].astype(BF16))
-        part = dot(jnp.concatenate(kept, axis=0), value_ref[span, :], 1, 0)
+        part = dot(jnp.concatenate(kept, axis=0), value_ref[span, lanes], 1, 0)
         if start:
             part += out_ref[start:, :]
         out_ref[start:, :] = part
@@ -87,17 +89,19 @@
             fill(wide_ref, bucket_refs[5 + level], 0, level, where_ref[level].astype(F32))
 
     columns = coef_ref[...].T
+    tile = out_ref.shape[0]
+    span = pl.ds(pl.multiple_of(pl.program_id(0) * tile, tile), tile)
     square = None
     for head in range(heads):
         lanes = slice(head * width, (head + 1) * width)
-        query = query_ref[:, lanes]
-        out = columns[:, head : head + 1] * local_ref[:, lanes]
+        query = query_ref[span, lanes]
+        out = columns[:, head : head + 1] * local_ref[span, lanes]
         for level in range(depth):
             read = dot(query, wide_ref[head, level * width : (level + 1) * width, :], 1, 0)
             place = (level + 1) * heads + head
             out += columns[:, place : place + 1] * read
         out_ref[:, lanes] = out
-        weighted = cot_ref[:, lanes].astype(F32) * gain_ref[:, lanes]
+        weighted = cot_ref[span, lanes].astype(F32) * gain_ref[:, lanes]
         square = out * out if square is None else square + out * out
         inner = weighted * out if head == 0 else inner + weighted * out
     sums_ref[0:1, :] = lane_sums(square)[0:1]
@@ -105,13 +109,14 @@
 
 
 def bucket_kernel(features, where_ref, query_ref, out_ref, cot_ref, gain_ref, coef_ref, sums_ref, *refs):
-    mixed_ref, half_ref, gain_out_ref = refs[:3]
-    mine0_ref, theirs0_ref, mine1_ref, theirs1_ref = refs[3:7]
-    quarter_refs, extra_refs, (total_ref, gain_total_ref) = refs[7:11], refs[11:-2], refs[-2:]
+    mixed_ref, half_ref = refs[:2]
+    mine0_ref, theirs0_ref, mine1_ref, theirs1_ref = refs[2:6]
+    quarter_refs, extra_refs, (total_ref, gain_total_ref) = refs[6:10], refs[10:-2], refs[-2:]
     heads, stacked, width = total_ref.shape
     depth = stacked // width
     step = pl.program_id(0)
-    tile = query_ref.shape[0]
+    tile = half_ref.shape[0]
+    span = pl.ds(pl.multiple_of(step * tile, tile), tile)
 
     @pl.when(step == 0)
     def _():
@@ -125,14 +130,14 @@
     factor = jnp.broadcast_to(columns[:, 1:2], (tile, width))
     for head in range(heads):
         lanes = slice(head * width, (head + 1) * width)
-        cot = cot_ref[:, lanes].astype(F32)
-        normed = out_ref[:, lanes] * inverse
+        cot = cot_ref[span, lanes].astype(F32)
+        normed = out_ref[span, lanes] * inverse
         gain = gain_ref[:, lanes]
         mixed_ref[:, lanes] = (normed * gain).astype(BF16)
         gain_total_ref[head] += jnp.sum((cot * normed).reshape(tile // 8, 8, width), axis=0)
         half = ((cot * gain) * inverse - normed * factor).astype(BF16)
         half_ref[:, lanes] = half
-        turned = query_ref[:, lanes].T.astype(F32)
+        turned = query_ref[span, lanes].T.astype(F32)
         stack = jnp.concatenate(
             [
                 (turned * coef_ref[(level + 1) * heads + head : (level + 1) * heads + head + 1, :]).astype(BF16)
@@ -146,9 +151,13 @@
     def _():
         low, high = where_ref[0], where_ref[1]
         quarter = heads // 4
+        blocks = quarter * width
+        for offset in range(4):
+            quarter_refs[offset][blocks:, :] = jnp.zeros_like(quarter_refs[offset][blocks:, :])
         for head in range(heads):
-            lanes = slice(head * width, (head + 1) * width)
-            gain_out_ref[:, lanes] = jnp.sum(gain_total_ref[head], axis=0, keepdims=True)
+            gain_row = jnp.sum(gain_total_ref[head], axis=0, keepdims=True)
+            for offset in range(4):
+                quarter_refs[offset][blocks + head : blocks + head + 1, :] = gain_row
             piece, inside, place = head // quarter, head % quarter, head % (2 * quarter)
             parts = [
                 total_ref[head, level * width : (level + 1) * width, :] * where_ref[level].astype(F32)
@@ -170,7 +179,7 @@
 
                 @pl.when(owner == piece)
                 def _():
-                    quarter_refs[offset][inside] = parts[2]
+                    quarter_refs[offset][inside * width : (inside + 1) * width, :] = parts[2]
 
             for level in range(3, depth):
                 extra_refs[level - 3][head] = parts[level]
@@ -183,7 +192,8 @@
     grad_query_ref, key_sum_ref, value_sum_ref, level_ref, pick_ref, key_acc, value_acc = refs
     levels = coef_ref.shape[0]
     head = base + pl.program_id(0)
-    rows, width = query_ref.shape
+    rows, width = key_acc.shape
+    lanes = pl.ds(pl.multiple_of(head * width, width), width)
     tile = min(TILE, rows)
 
     @pl.when(pl.program_id(0) == 0)
@@ -204,11 +214,11 @@
     for start in range(0, rows, tile):
         span = slice(start, start + tile)
         stop = start + tile
-        query = query_ref[span, :]
-        half = half_ref[span, :]
+        query = query_ref[span, lanes]
+        half = half_ref[span, lanes]
         grad = half.astype(F32)
         wide_query = query.astype(F32)
-        products = [(grad * local_ref[span, :]).astype(BF16)]
+        products = [(grad * local_ref[span, lanes]).astype(BF16)]
         query_sum = None
         for level in range(levels - 1):
             read = dot(half, wide_ref[0, level * width : (level + 1) * width, :], 1, 1)
@@ -220,8 +230,8 @@
             level_ref[level, pl.ds(head, 1), span] = sums[level : level + 1, :]
 
         weighted = (columns[span, 0:1] * grad).astype(BF16)
-        scores = dot(key_ref[:stop, :], query, 1, 1)
-        pair = dot(value_ref[:stop, :], half, 1, 1) * first_row[:, span]
+        scores = dot(key_ref[:stop, lanes], query, 1, 1)
+        pair = dot(value_ref[:stop, lanes], half, 1, 1) * first_row[:, span]
         kept = [jnp.where(keep, scores[start:], 0.0).astype(BF16)]
         pairs = [jnp.where(keep, pair[start:], 0.0).astype(BF16)]
         if start:
@@ -236,23 +246,55 @@
             key_acc[:start, :] += key_part[:start]
         value_acc[span, :] = value_part[start:]
         key_acc[span, :] = key_part[start:]
-        grad_query_ref[span, :] = (query_sum + dot(pairs, key_ref[:stop, :], 0, 0)).astype(BF16)
+        grad_query_ref[span, :] = (query_sum + dot(pairs, key_ref[:stop, lanes], 0, 0)).astype(BF16)
     key_sum_ref[...] = key_acc[...]
     value_sum_ref[...] = value_acc[...]
+
+
+def lower_kernel(where_ref, near_ref, far_ref, mine_ref, swapped_ref, out_ref):
+    half, width, _ = mine_ref.shape
+    quarter = half // 2
+    blocks = quarter * width
+    for index in range(half):
+        source, place = (near_ref, index) if index < quarter else (far_ref, index - quarter)
+        rows = slice(index * width, (index + 1) * width)
+        out_ref[rows, :] = source[place * width : (place + 1) * width, :] + (
+            mine_ref[index] + swapped_ref[index]
+        )
+    both = where_ref[1] * where_ref[2] == 1
+    out_ref[2 * blocks :, :] = jnp.where(both, far_ref[blocks:, :], near_ref[blocks:, :])
+
+
+def own_kernel(where_ref, near_ref, far_ref, down_ref, mine_ref, sum_ref, lowered_ref, own_ref, send_ref, gain_ref):
+    half, width, _ = mine_ref.shape
+    quarter = half // 2
+    blocks = quarter * width
+    for index in range(half):
+        source, place = (near_ref, index) if index < quarter else (far_ref, index - quarter)
+        own = source[place * width : (place + 1) * width, :] + down_ref[
+            index * width : (index + 1) * width, :
+        ]
+        own_ref[index] = own
+        send_ref[index] = own + mine_ref[index]
+    kept = where_ref[1] + where_ref[2] > 0
+    gain_ref[...] = sum_ref[blocks:, :] + jnp.where(
+        kept, lowered_ref[2 * blocks :, :], down_ref[2 * blocks :, :]
+    )
 
 
 def final_kernel(where_ref, key_ref, value_ref, key_sum_ref, value_sum_ref, own_ref, add_ref, other_ref, *refs):
     extra, (key_out_ref, value_out_ref) = refs[:-2], refs[-2:]
     head = pl.program_id(0)
-    half = own_ref.shape[0]
+    half, width, _ = own_ref.shape
     place = head % half
+    lanes = pl.ds(pl.multiple_of(head * width, width), width)
     mine = head // half == where_ref[0]
     state = jnp.where(mine, own_ref[place] + add_ref[place], other_ref[place])
     if extra:
         state += extra[0][head]
     state = state.astype(BF16)
-    key_out_ref[...] = (key_sum_ref[...] + dot(value_ref[...], state, 1, 1)).astype(BF16)
-    value_out_ref[...] = (value_sum_ref[...] + dot(key_ref[...], state, 1, 0)).astype(BF16)
+    key_out_ref[...] = (key_sum_ref[:, lanes] + dot(value_ref[:, lanes], state, 1, 1)).astype(BF16)
+    value_out_ref[...] = (value_sum_ref[:, lanes] + dot(key_ref[:, lanes], state, 1, 0)).astype(BF16)
 
 
 def send(block, count, mask, keep=lambda place: True):
@@ -281,7 +323,9 @@
     def shaped(*shape, dtype=F32):
         return jax.ShapeDtypeStruct(shape, dtype)
 
-    def call(kernel, name, grid, flops, moved, in_specs, out_specs, out_shape, scratch=(), aliases=None):
+    def call(
+        kernel, name, grid, flops, moved, in_specs, out_specs, out_shape, scratch=(), aliases=None
+    ):
         return pl.pallas_call(
             kernel,
             grid_spec=pltpu.PrefetchScalarGridSpec(
@@ -300,6 +344,17 @@
             cost_estimate=pl.CostEstimate(flops=flops, bytes_accessed=moved, transcendentals=0),
         )
 
+    def small(kernel, name, operands, out_shape):
+        return pl.pallas_call(
+            kernel,
+            in_specs=[pl.BlockSpec(memory_space=pltpu.SMEM)] + [pl.BlockSpec(memory_space=pltpu.VMEM)] * operands,
+            out_specs=jax.tree.map(lambda _: pl.BlockSpec(memory_space=pltpu.VMEM), out_shape),
+            out_shape=out_shape,
+            name=name,
+            compiler_params=pltpu.CompilerParams(vmem_limit_bytes=VMEM_LIMIT),
+            cost_estimate=pl.CostEstimate(flops=size, bytes_accessed=size, transcendentals=0),
+        )
+
     def states(mine):
         at = spec(
             (rows, width),
@@ -316,6 +371,8 @@
             shaped(half, width, width),
         )(where, key, value)
 
+    resident = pl.BlockSpec(memory_space=pltpu.VMEM)
+
     def bit(place, level):
         return place >> level & 1
 
@@ -331,24 +388,37 @@
     quarter_f32 = shaped(quarter, width, width)
     full_f32 = shaped(heads, width, width)
 
+    def across(tile):
+        return spec((tile, heads * width), lambda h, where: (h, 0))
+
+    def along(count, tile):
+        return spec((count, tile), lambda h, where: (0, h))
+
     theirs = states(False)
     first = send(theirs, count, 1)
     mine = states(True)
 
-    local = call(
-        local_kernel,
-        "local",
-        heads,
-        3 * rows * size,
-        10 * size,
-        [token, token, token],
-        token,
-        token_f32,
-    )(where, query, key, value)
-
+    def local_part(piece, previous):
+        base = piece * half
+        at = spec((rows, width), lambda h, where: (0, base + h))
+        return call(
+            functools.partial(local_kernel, base),
+            "local",
+            half,
+            3 * rows * size // 2,
+            10 * size // 2,
+            [resident] * 3 + [pl.BlockSpec(memory_space=pl.ANY)] * len(previous),
+            at,
+            token_f32,
+            aliases={4: 0} if previous else {},
+        )(where, query, key, value, *previous)
+
+    local = local_part(0, [])
     first_rest = send(mine, count, 1, lambda g: not bit(g, 0))
     pair = mine + first
     second = send(pair, count, 2, lambda g: not bit(g, 1))
+    second, local = lax.optimization_barrier((second, local))
+    local = local_part(1, [local])
     second_rest = send(second, count, 1, lambda g: bit(g, 1))
     four = pair + second
     near = send(four[:quarter], count, 6, lambda g: bit(g, 1) and not bit(g, 2))
@@ -370,12 +440,6 @@
 
     coef_rows = level_coef.reshape(-1, rows)
 
-    def across(tile):
-        return spec((tile, heads * width), lambda h, where: (h, 0))
-
-    def along(count, tile):
-        return spec((count, tile), lambda h, where: (0, h))
-
     tile = min(TILE // 2, rows)
     output, sums, wide = call(
         output_kernel,
@@ -383,14 +447,20 @@
         rows // tile,
         2 * depth * square,
         12 * size,
-        [across(tile)] * 3 + [whole(1, heads * width), along(coef_rows.shape[0], tile)] + bucket_specs,
+        [resident] * 3 + [whole(1, heads * width), along(coef_rows.shape[0], tile)] + bucket_specs,
         [across(tile), along(2, tile), whole(heads, depth * width, width)],
         [token_f32, shaped(2, rows), shaped(heads, depth * width, width, dtype=BF16)],
     )(where, query, local, cotangent, gain_row, coef_rows, *buckets)
 
-    total = lax.psum(sums, "head")
+    total = sums
+    step = 1
+    while step < heads_all:
+        total = total + lax.ppermute(total, "head", [(g, g ^ step) for g in range(heads_all)])
+        step *= 2
 
     extra_count = max(depth - 3, 0)
+    blocks = quarter * width
+    carrying = (blocks + -(-heads // 8) * 8, width)
     tile = min(TILE, rows)
     grads = call(
         functools.partial(bucket_kernel, features),
@@ -398,25 +468,24 @@
         rows // tile,
         2 * depth * square,
         10 * size,
-        [across(tile)] * 3 + [whole(1, heads * width), along(coef_rows.shape[0], tile), along(2, tile)],
+        [resident] * 3 + [whole(1, heads * width), along(coef_rows.shape[0], tile), along(2, tile)],
         [across(tile)] * 2
-        + [whole(1, heads * width)]
         + [half_spec] * 4
-        + [quarter_spec] * 4
+        + [whole(*carrying)] * 4
         + [full_spec] * extra_count,
-        [token_bf16, token_bf16, shaped(1, heads * width)]
+        [token_bf16, token_bf16]
         + [half_f32] * 4
-        + [quarter_f32] * 4
+        + [shaped(*carrying)] * 4
         + [full_f32] * extra_count,
         [pltpu.VMEM((heads, depth * width, width), F32), pltpu.VMEM((heads, 8, width), F32)],
     )(where, query, output, cotangent, gain_row, coef_rows, total)
-    mixed, grad_half, gain_part, mine0, theirs0, mine1, theirs1 = grads[:7]
-    quarters, extra = grads[7:11], grads[11:]
+    mixed, grad_half, mine0, theirs0, mine1, theirs1 = grads[:6]
+    quarters, extra = grads[6:10], grads[10:]
 
     def main(piece, previous):
         base = piece * quarter
         at = spec((rows, width), lambda h, where: (0, base + h))
-        ins = [at] * 5 + [
+        ins = [resident] * 5 + [
             coef_spec,
             spec((1, depth * width, width), lambda h, where: (base + h, 0, 0)),
         ]
@@ -424,7 +493,7 @@
         if previous:
             aliases = {1 + len(ins) + index: index for index in range(3)}
             ins += [pl.BlockSpec(memory_space=pl.ANY)] * 3 + [coef_spec]
-        return call(
+        return list(call(
             functools.partial(main_kernel, base),
             "main",
             quarter,
@@ -435,23 +504,32 @@
             [token_bf16, token_f32, token_f32, shaped(*level_coef.shape)],
             [pltpu.VMEM(((depth + 1) * width, width), BF16)] + [pltpu.VMEM((rows, width), F32)] * 2,
             aliases,
-        )(where, query, key, value, local, grad_half, level_coef, wide, *previous)
-
+        )(where, query, key, value, local, grad_half, level_coef, wide, *previous))
+
+    sent = [send(quarters[mask], count, mask) for mask in (1, 2, 3)]
     swapped = send(theirs1, count, 1, lambda g: bit(g, 1))
-    gathered = quarters[0]
-    for mask in (1, 2, 3):
-        gathered = gathered + send(quarters[mask], count, mask, lambda g: bit(g, 2))
-    near = send(gathered, count, 6, lambda g: bit(g, 2) and not bit(g, 1))
-    far = send(gathered, count, 4, lambda g: bit(g, 2) and bit(g, 1))
-    four = jnp.concatenate([near, far])
-    down = send(four + mine1 + swapped, count, 2, lambda g: bit(g, 1))
+    results = main(0, [])
+    sent, swapped, results[-1] = lax.optimization_barrier((sent, swapped, results[-1]))
+    gathered = (quarters[0] + sent[0]) + (sent[1] + sent[2])
+    near = send(gathered, count, 6, lambda g: bit(g, 1) != bit(g, 2))
+    far = send(gathered, count, 4, lambda g: bit(g, 1))
+    results = main(1, results)
+    near, far, results[-1] = lax.optimization_barrier((near, far, results[-1]))
+    lowered = small(
+        lower_kernel, "lower", 4, shaped(2 * blocks + carrying[0] - blocks, width)
+    )(where, near, far, mine1, swapped)
+    down = send(lowered, count, 2, lambda g: bit(g, 1))
     add = send(theirs0, count, 1, lambda g: bit(g, 0))
-    own = four + down
-    other = send(own + mine0, count, 1)
-
-    grad_gain = gain_part.reshape(-1)
-    for level in range(depth):
+    results = main(2, results)
+    down, results[-1] = lax.optimization_barrier((down, results[-1]))
+    own, moved, gain_sum = small(
+        own_kernel, "own", 6, [half_f32, half_f32, shaped(carrying[0] - blocks, width)]
+    )(where, near, far, down, mine0, gathered, lowered)
+    other = send(moved, count, 1)
+    grad_gain = gain_sum[:heads].reshape(-1)
+    for level in range(3, depth):
         grad_gain = grad_gain + send(grad_gain, count, 1 << level)
+    results = main(3, results)
 
     carried = []
     if depth > 3:
@@ -462,9 +540,6 @@
             block = block + send(block, count, 1 << level)
         carried = [block]
 
-    results = []
-    for piece in range(4):
-        results = main(piece, results)
     grad_query, key_sum, value_sum, grad_level = results
 
     grad_key, grad_value = call(
@@ -473,7 +548,7 @@
         heads,
         4 * square,
         16 * size,
-        [token, token, token, token] + [half_spec] * 3 + [full_spec] * len(carried),
+        [resident] * 4 + [half_spec] * 3 + [full_spec] * len(carried),
         [token, token],
         [token_bf16, token_bf16],
     )(where, key, value, key_sum, value_sum, own, add, other, *carried)

time: 152 us -> 123 us (0.81)
  the two profiles are of different devices: /device:TPU:0 before, /device:TPU:24 now
where the time goes in v3:
time: 123 us
  Pallas kernels  65.4 us (53%)
  starting transfers between devices  41.5 us (34%)
  waiting for transfers between devices  11.7 us (10%)
  local copies, waits for them, and re-layouts  3.24 us (3%)
    ppermute x18, starting transfers between devices, send(): lax.ppermute(block, 'seq', [(g, g ^ mask) for g in range(count) if keep(g)])  40 us
    pallas_call x4, Pallas kernels, main(): call(functools.partial(main_kernel, base), 'main', quarter, (8 * rows * s...  29.1 us
    pallas_call x2, Pallas kernels, local_part(): call(functools.partial(local_kernel, base), 'local', half, 3 * rows * siz...  9.16 us
    pallas_call x1, Pallas kernels, body(): call(output_kernel, 'output', rows // tile, 2 * depth * square, 12 * size...  8.98 us
    ppermute x18, waiting for transfers between devices, send(): lax.ppermute(block, 'seq', [(g, g ^ mask) for g in range(count) if keep(g)])  8.39 us
    pallas_call x1, Pallas kernels, body(): call(functools.partial(bucket_kernel, features), 'buckets', rows // tile,...  6.47 us
    pallas_call x1, Pallas kernels, body(): call(final_kernel, 'final', heads, 4 * square, 16 * size, [resident] * 4...  5.37 us
    pallas_call x2, Pallas kernels, states(): call(states_kernel, 'states', half, square, 2 * size, [at, at], spec((1,...  4.56 us
  transfers between devices with their start and end apart: 20, of which 6 were waited for; matrix products, arithmetic and copies ran while one was open for 0% of the time, Pallas kernels for 34%

profile of v3, /device:TPU:24, one launch (start us, length us, event | category | flops | bytes accessed | tf_op | source)
XLA Modules:
  0.0 123.0 jit_solution(12989945241949996897)
XLA Ops:
  0.8 1.6 %copy-done = bf16[1024,1024]{1,0:T(8,128)(2,1)S(1)} copy-done((bf16[1024,1024]{1,0:T(8,128)(2,1)S(1)}, bf16[1024,1024]{1,0:T(8,128)(2,1)}, u32[]{:S(2)}) %copy-start) | copy-done | bytes 2097176
  2.4 1.6 %copy-done.2 = bf16[1024,1024]{1,0:T(8,128)(2,1)S(1)} copy-done((bf16[1024,1024]{1,0:T(8,128)(2,1)S(1)}, bf16[1024,1024]{1,0:T(8,128)(2,1)}, u32[]{:S(2)}) %copy-start.2) | copy-done | bytes 2097176
  3.9 2.3 %states.3 = f32[4,128,128]{2,1,0:T(8,128)S(1)} custom-call(s32[3]{0:T(128)S(1)} %pad_add_fusion.where_ref, bf16[1024,1024]{1,0:T(8,128)(2,1)S(1)} %copy-done, bf16[1024,1024]{1,0:T(8,128)(2,1)S(1)} %copy-done.2), custom_call_target="tpu_custom_call" | custom-call | flops 134217728 | bytes 2097152 | tf_op jit(solution)/shard_map/states/pallas_call | solution.py:363
  6.3 1.6 %collective-permute-start = (f32[4,128,128]{2,1,0:T(8,128)S(1)}, f32[4,128,128]{2,1,0:T(8,128)S(1)}, u32[]{:S(2)}, u32[]{:S(2)}) collective-permute-start(f32[4,128,128]{2,1,0:T(8,128)S(1)} %states.3), channel_id=1, source_target_pairs={{0,4},{4,0},{8,12},{12,8},{16,20},{20,16},{24,28},{28,24},{1,5},{5... | collective-permute-start | bytes 786440 | tf_op jit(solution)/shard_map/ppermute | solution.py:301
  7.8 2.3 %states.2 = f32[4,128,128]{2,1,0:T(8,128)S(1)} custom-call(s32[3]{0:T(128)S(1)} %pad_add_fusion.where_ref, bf16[1024,1024]{1,0:T(8,128)(2,1)S(1)} %copy-done, bf16[1024,1024]{1,0:T(8,128)(2,1)S(1)} %copy-done.2), custom_call_target="tpu_custom_call" | custom-call | flops 134217728 | bytes 2097152 | tf_op jit(solution)/shard_map/states/pallas_call | solution.py:363
  10.1 4.2 %collective-permute-done.refs_0_ = f32[4,128,128]{2,1,0:T(8,128)S(1)} collective-permute-done((f32[4,128,128]{2,1,0:T(8,128)S(1)}, f32[4,128,128]{2,1,0:T(8,128)S(1)}, u32[]{:S(2)}, u32[]{:S(2)}) %collective-permute-start) | collective-permute-done | bytes 262176 | tf_op jit(solution)/shard_map/ppermute | solution.py:301
  14.4 1.3 %collective-permute-start.1 = (f32[4,128,128]{2,1,0:T(8,128)S(1)}, f32[4,128,128]{2,1,0:T(8,128)S(1)}, u32[]{:S(2)}, u32[]{:S(2)}) collective-permute-start(f32[4,128,128]{2,1,0:T(8,128)S(1)} %add.40), channel_id=1, source_target_pairs={{0,8},{4,12},{16,24},{20,28},{1,9},{5,13},{17,25},{21,29},{2,10},{... | collective-permute-start | bytes 786440 | tf_op jit(solution)/shard_map/ppermute | solution.py:301
  15.7 4.6 %local.2.refs_0_ = f32[1024,1024]{1,0:T(8,128)S(1)} custom-call(s32[3]{0:T(128)S(1)} %pad_add_fusion.where_ref, bf16[1024,1024]{1,0:T(8,128)(2,1)S(1)} %copy-done.4, bf16[1024,1024]{1,0:T(8,128)(2,1)S(1)} %copy-done.1, bf16[1024,1024]{1,0:T(8,128)(2,1)S(1)} %copy-done.2), custom_call_target="tpu_custom_call" | custom-call | flops 1610612736 | bytes 5242880 | tf_op jit(solution)/shard_map/local/pallas_call | solution.py:404
  20.3 3.2 %collective-permute-done.1.refs_2_ = f32[4,128,128]{2,1,0:T(8,128)S(1)} collective-permute-done((f32[4,128,128]{2,1,0:T(8,128)S(1)}, f32[4,128,128]{2,1,0:T(8,128)S(1)}, u32[]{:S(2)}, u32[]{:S(2)}) %collective-permute-start.1) | collective-permute-done | bytes 262176 | tf_op jit(solution)/shard_map/ppermute | solution.py:301
  23.6 1.3 %collective-permute-start.5 = (f32[2,128,128]{2,1,0:T(8,128)S(1)}, f32[2,128,128]{2,1,0:T(8,128)S(1)}, u32[]{:S(2)}, u32[]{:S(2)}) collective-permute-start(f32[2,128,128]{2,1,0:T(8,128)S(1)} %get-tuple-element.98), channel_id=1, source_target_pairs={{8,24},{12,28},{9,25},{13,29},{10,26},{14,30},{11,27},{15,31}} | collective-permute-start | bytes 393224 | tf_op jit(solution)/shard_map/ppermute | solution.py:301
  25.5 3.4 %collective-permute-start.2 = (f32[4,128,128]{2,1,0:T(8,128)S(1)}, f32[4,128,128]{2,1,0:T(8,128)S(1)}, u32[]{:S(2)}, u32[]{:S(2)}) collective-permute-start(f32[4,128,128]{2,1,0:T(8,128)S(1)} %states.2), channel_id=1, source_target_pairs={{0,4},{8,12},{16,20},{24,28},{1,5},{9,13},{17,21},{25,29},{2,6},{1... | collective-permute-start | bytes 786440 | tf_op jit(solution)/shard_map/ppermute | solution.py:301
  29.0 1.9 %collective-permute-start.3 = (f32[4,128,128]{2,1,0:T(8,128)S(1)}, f32[4,128,128]{2,1,0:T(8,128)S(1)}, u32[]{:S(2)}, u32[]{:S(2)}) collective-permute-start(f32[4,128,128]{2,1,0:T(8,128)S(1)} %collective-permute-done.1.refs_2_), channel_id=1, source_target_pairs={{8,12},{12,8},{24,28},{28,24},{9,13},{13,9},{25,29},{29,25},{10,14... | collective-permute-start | bytes 786440 | tf_op jit(solution)/shard_map/ppermute | solution.py:301
  31.4 5.0 %collective-permute-start.8 = (f32[2,128,128]{2,1,0:T(8,128)S(1)}, f32[2,128,128]{2,1,0:T(8,128)S(1)}, u32[]{:S(2)}, u32[]{:S(2)}) collective-permute-start(f32[2,128,128]{2,1,0:T(8,128)S(1)} %add.42.refs_4_), channel_id=1, source_target_pairs={{16,28},{20,24},{24,20},{28,16},{17,29},{21,25},{25,21},{29,17},{1... | collective-permute-start | bytes 393224 | tf_op jit(solution)/shard_map/ppermute | solution.py:301
  36.3 2.1 %collective-permute-start.7 = (f32[2,128,128]{2,1,0:T(8,128)S(1)}, f32[2,128,128]{2,1,0:T(8,128)S(1)}, u32[]{:S(2)}, u32[]{:S(2)}) collective-permute-start(f32[2,128,128]{2,1,0:T(8,128)S(1)} %add.42.refs_4_), channel_id=1, source_target_pairs={{16,24},{20,28},{24,16},{28,20},{17,25},{21,29},{25,17},{29,21},{1... | collective-permute-start | bytes 393224 | tf_op jit(solution)/shard_map/ppermute | solution.py:301
  38.4 2.3 %collective-permute-start.6 = (f32[2,128,128]{2,1,0:T(8,128)S(1)}, f32[2,128,128]{2,1,0:T(8,128)S(1)}, u32[]{:S(2)}, u32[]{:S(2)}) collective-permute-start(f32[2,128,128]{2,1,0:T(8,128)S(1)} %add.42.refs_4_), channel_id=1, source_target_pairs={{16,20},{20,16},{24,28},{28,24},{17,21},{21,17},{25,29},{29,25},{1... | collective-permute-start | bytes 393224 | tf_op jit(solution)/shard_map/ppermute | solution.py:301
  40.8 4.6 %local.3.local_ref = f32[1024,1024]{1,0:T(8,128)S(1)} custom-call(s32[3]{0:T(128)S(1)} %pad_add_fusion.where_ref, bf16[1024,1024]{1,0:T(8,128)(2,1)S(1)} %copy-done.4, bf16[1024,1024]{1,0:T(8,128)(2,1)S(1)} %copy-done.1, bf16[1024,1024]{1,0:T(8,128)(2,1)S(1)} %copy-done.2, f32[1024,1024]{1,0:T(8,128)S(1)} %local.2.refs_0_), custom_call_target="tpu_custom_call", output_to_operand_aliasing={{}: (4, {})} | custom-call | flops 1610612736 | bytes 5242880 | tf_op jit(solution)/shard_map/local/pallas_call | solution.py:404
  45.4 9.0 %output.1 = (f32[1024,1024]{1,0:T(8,128)S(1)}, f32[2,1024]{1,0:T(2,128)S(1)}, bf16[8,384,128]{2,1,0:T(8,128)(2,1)S(1)}) custom-call(s32[3]{0:T(128)S(1)} %pad_add_fusion.where_ref, bf16[1024,1024]{1,0:T(8,128)(2,1)S(1)} %copy-done.4, f32[1024,1024]{1,0:T(8,128)S(1)} %local.3.local_ref, bf16[1024,1024]{1,0:T(8,128)(2,1)S(1)} %copy-done.5, ...), custom_call_target="tpu_custom_call" | custom-call | flops 805306368 | bytes 12582912 | tf_op jit(solution)/shard_map/output/pallas_call | solution.py:444
  54.4 1.2 collective-permute-done.9
  55.6 1.5 %collective-permute-start.10 = (f32[2,1024]{1,0:T(2,128)S(1)}, f32[2,1024]{1,0:T(2,128)S(1)}, u32[]{:S(2)}, u32[]{:S(2)}) collective-permute-start(f32[2,1024]{1,0:T(2,128)S(1)} %add.43), channel_id=1, source_target_pairs={{0,2},{1,3},{2,0},{3,1},{4,6},{5,7},{6,4},{7,5},{8,10},{9,11},{10,... | collective-permute-start | bytes 24584 | tf_op jit(solution)/shard_map/ppermute | solution.py:458
  57.1 2.2 %collective-permute-done.10 = f32[2,1024]{1,0:T(2,128)S(1)} collective-permute-done((f32[2,1024]{1,0:T(2,128)S(1)}, f32[2,1024]{1,0:T(2,128)S(1)}, u32[]{:S(2)}, u32[]{:S(2)}) %collective-permute-start.10) | collective-permute-done | bytes 8224 | tf_op jit(solution)/shard_map/ppermute | solution.py:458
  59.3 6.5 %buckets.1 = (bf16[1024,1024]{1,0:T(8,128)(2,1)}, bf16[1024,1024]{1,0:T(8,128)(2,1)S(1)}, f32[4,128,128]{2,1,0:T(8,128)S(1)}, f32[4,128,128]{2,1,0:T(8,128)S(1)}...) custom-call(s32[3]{0:T(128)S(1)} %pad_add_fusion.where_ref, ...), custom_call_target="tpu_custom_call" | custom-call | flops 805306368 | bytes 10485760 | tf_op jit(solution)/shard_map/buckets/pallas_call | solution.py:465
  65.7 3.5 %collective-permute-start.14 = (f32[4,128,128]{2,1,0:T(8,128)S(1)}, f32[4,128,128]{2,1,0:T(8,128)S(1)}, u32[]{:S(2)}, u32[]{:S(2)}) collective-permute-start(f32[4,128,128]{2,1,0:T(8,128)S(1)} %get-tuple-element.65), channel_id=1, source_target_pairs={{8,12},{12,8},{24,28},{28,24},{9,13},{13,9},{25,29},{29,25},{10,14... | collective-permute-start | bytes 786440 | tf_op jit(solution)/shard_map/ppermute | solution.py:301
  69.9 2.9 %collective-permute-start.13 = (f32[264,128]{1,0:T(8,128)S(1)}, f32[264,128]{1,0:T(8,128)S(1)}, u32[]{:S(2)}, u32[]{:S(2)}) collective-permute-start(f32[264,128]{1,0:T(8,128)S(1)} %get-tuple-element.64), channel_id=1, source_target_pairs={{0,12},{4,8},{8,4},{12,0},{16,28},{20,24},{24,20},{28,16},{1,13},{... | collective-permute-start | bytes 405512 | tf_op jit(solution)/shard_map/ppermute | solution.py:301
  72.8 7.3 %main.4 = (bf16[1024,1024]{1,0:T(8,128)(2,1)}, f32[1024,1024]{1,0:T(8,128)S(1)}, f32[1024,1024]{1,0:T(8,128)S(1)}, f32[4,8,1024]{2,1,0:T(8,128)S(1)}) custom-call(s32[3]{0:T(128)S(1)} %pad_add_fusion.where_ref, bf16[1024,1024]{1,0:T(8,128)(2,1)S(1)} %copy-done.4, bf16[1024,1024]{1,0:T(8,128)(2,1)S(1)} %copy-done.1, bf16[1024,1024]{1,0:T(8,128)(2,1)S(1)} %copy-done.3, ...), custom_call_target="tpu_custom_call" | custom-call | flops 2550136832 | bytes 5767168 | tf_op jit(solution)/shard_map/main/pallas_call | solution.py:496
  80.7 1.9 %collective-permute-start.16 = (f32[264,128]{1,0:T(8,128)S(1)}, f32[264,128]{1,0:T(8,128)S(1)}, u32[]{:S(2)}, u32[]{:S(2)}) collective-permute-start(f32[264,128]{1,0:T(8,128)S(1)} %add_add_fusion.sum_ref), channel_id=1, source_target_pairs={{8,24},{12,28},{24,8},{28,12},{9,25},{13,29},{25,9},{29,13},{10,26... | collective-permute-start | bytes 405512 | tf_op jit(solution)/shard_map/ppermute | solution.py:301
  83.5 7.3 %main.5 = (bf16[1024,1024]{1,0:T(8,128)(2,1)}, f32[1024,1024]{1,0:T(8,128)S(1)}, f32[1024,1024]{1,0:T(8,128)S(1)}, f32[4,8,1024]{2,1,0:T(8,128)S(1)}) custom-call(s32[3]{0:T(128)S(1)} %pad_add_fusion.where_ref, bf16[1024,1024]{1,0:T(8,128)(2,1)S(1)} %copy-done.4, ...), custom_call_target="tpu_custom_call", output_to_operand_aliasing={{0}: (8, {}), {1}: (9, {}), {2}: (10, {})} | custom-call | flops 2550136832 | bytes 5767168 | tf_op jit(solution)/shard_map/main/pallas_call | solution.py:496
  91.4 6.6 %collective-permute-start.17 = (f32[520,128]{1,0:T(8,128)S(1)}, f32[520,128]{1,0:T(8,128)S(1)}, u32[]{:S(2)}, u32[]{:S(2)}) collective-permute-start(f32[520,128]{1,0:T(8,128)S(1)} %lower.1.lowered_ref), channel_id=1, source_target_pairs={{8,0},{12,4},{24,16},{28,20},{9,1},{13,5},{25,17},{29,21},{10,2},{... | collective-permute-start | bytes 798728 | tf_op jit(solution)/shard_map/ppermute | solution.py:301
  98.0 1.3 %collective-permute-start.18 = (f32[4,128,128]{2,1,0:T(8,128)S(1)}, f32[4,128,128]{2,1,0:T(8,128)S(1)}, u32[]{:S(2)}, u32[]{:S(2)}) collective-permute-start(f32[4,128,128]{2,1,0:T(8,128)S(1)} %get-tuple-element.92), channel_id=1, source_target_pairs={{4,0},{12,8},{20,16},{28,24},{5,1},{13,9},{21,17},{29,25},{6,2},{1... | collective-permute-start | bytes 786440 | tf_op jit(solution)/shard_map/ppermute | solution.py:301
  99.3 7.3 %main.6 = (bf16[1024,1024]{1,0:T(8,128)(2,1)}, f32[1024,1024]{1,0:T(8,128)S(1)}, f32[1024,1024]{1,0:T(8,128)S(1)}, f32[4,8,1024]{2,1,0:T(8,128)S(1)}) custom-call(s32[3]{0:T(128)S(1)} %pad_add_fusion.where_ref, bf16[1024,1024]{1,0:T(8,128)(2,1)S(1)} %copy-done.4, ...), custom_call_target="tpu_custom_call", output_to_operand_aliasing={{0}: (8, {}), {1}: (9, {}), {2}: (10, {})} | custom-call | flops 2550136832 | bytes 5767168 | tf_op jit(solution)/shard_map/main/pallas_call | solution.py:496
  107.7 2.7 %collective-permute-start.19 = (f32[4,128,128]{2,1,0:T(8,128)S(1)}, f32[4,128,128]{2,1,0:T(8,128)S(1)}, u32[]{:S(2)}, u32[]{:S(2)}) collective-permute-start(f32[4,128,128]{2,1,0:T(8,128)S(1)} %get-tuple-element.93), channel_id=1, source_target_pairs={{0,4},{4,0},{8,12},{12,8},{16,20},{20,16},{24,28},{28,24},{1,5},{5... | collective-permute-start | bytes 786440 | tf_op jit(solution)/shard_map/ppermute | solution.py:301
  110.4 7.2 %main.7 = (bf16[1024,1024]{1,0:T(8,128)(2,1)}, f32[1024,1024]{1,0:T(8,128)S(1)}, f32[1024,1024]{1,0:T(8,128)S(1)}, f32[4,8,1024]{2,1,0:T(8,128)}) custom-call(s32[3]{0:T(128)S(1)} %pad_add_fusion.where_ref, bf16[1024,1024]{1,0:T(8,128)(2,1)S(1)} %copy-done.4, ...), custom_call_target="tpu_custom_call", output_to_operand_aliasing={{0}: (8, {}), {1}: (9, {}), {2}: (10, {})} | custom-call | flops 2550136832 | bytes 5767168 | tf_op jit(solution)/shard_map/main/pallas_call | solution.py:496
  117.7 5.4 %final.1 = (bf16[1024,1024]{1,0:T(8,128)(2,1)}, bf16[1024,1024]{1,0:T(8,128)(2,1)}) custom-call(s32[3]{0:T(128)S(1)} %pad_add_fusion.where_ref, bf16[1024,1024]{1,0:T(8,128)(2,1)S(1)} %copy-done.1, bf16[1024,1024]{1,0:T(8,128)(2,1)S(1)} %copy-done.3, f32[1024,1024]{1,0:T(8,128)S(1)} %get-tuple-element.87.key_sum_ref, ...), custom_call_target="tpu_custom_call" | custom-call | flops 536870912 | bytes 16777216 | tf_op jit(solution)/shard_map/final/pallas_call | solution.py:545
  (45 shorter events, 5.2 us)
Async XLA Ops:
  0.8 1.6 %copy-start = (bf16[1024,1024]{1,0:T(8,128)(2,1)S(1)}, bf16[1024,1024]{1,0:T(8,128)(2,1)}, u32[]{:S(2)}) copy-start(bf16[1024,1024]{1,0:T(8,128)(2,1)} %key_ref.17) | copy-start | bytes 6291460
  2.4 1.6 %copy-start.2 = (bf16[1024,1024]{1,0:T(8,128)(2,1)S(1)}, bf16[1024,1024]{1,0:T(8,128)(2,1)}, u32[]{:S(2)}) copy-start(bf16[1024,1024]{1,0:T(8,128)(2,1)} %value_ref.17) | copy-start | bytes 6291460
  6.2 9.5 %copy-start.1 = (bf16[1024,1024]{1,0:T(8,128)(2,1)S(1)}, bf16[1024,1024]{1,0:T(8,128)(2,1)}, u32[]{:S(2)}) copy-start(bf16[1024,1024]{1,0:T(8,128)(2,1)} %key_ref.17) | copy-start | bytes 6291460
  6.2 9.5 %copy-start.4 = (bf16[1024,1024]{1,0:T(8,128)(2,1)S(1)}, bf16[1024,1024]{1,0:T(8,128)(2,1)}, u32[]{:S(2)}) copy-start(bf16[1024,1024]{1,0:T(8,128)(2,1)} %query_ref.15) | copy-start | bytes 6291460
  6.3 8.1 %collective-permute-start = (f32[4,128,128]{2,1,0:T(8,128)S(1)}, f32[4,128,128]{2,1,0:T(8,128)S(1)}, u32[]{:S(2)}, u32[]{:S(2)}) collective-permute-start(f32[4,128,128]{2,1,0:T(8,128)S(1)} %states.3), channel_id=1, source_target_pairs={{0,4},{4,0},{8,12},{12,8},{16,20},{20,16},{24,28},{28,24},{1,5},{5... | collective-permute-start | bytes 786440 | tf_op jit(solution)/shard_map/ppermute | solution.py:301
  14.4 9.1 %collective-permute-start.1 = (f32[4,128,128]{2,1,0:T(8,128)S(1)}, f32[4,128,128]{2,1,0:T(8,128)S(1)}, u32[]{:S(2)}, u32[]{:S(2)}) collective-permute-start(f32[4,128,128]{2,1,0:T(8,128)S(1)} %add.40), channel_id=1, source_target_pairs={{0,8},{4,12},{16,24},{20,28},{1,9},{5,13},{17,25},{21,29},{2,10},{... | collective-permute-start | bytes 786440 | tf_op jit(solution)/shard_map/ppermute | solution.py:301
  23.6 7.8 %collective-permute-start.5 = (f32[2,128,128]{2,1,0:T(8,128)S(1)}, f32[2,128,128]{2,1,0:T(8,128)S(1)}, u32[]{:S(2)}, u32[]{:S(2)}) collective-permute-start(f32[2,128,128]{2,1,0:T(8,128)S(1)} %get-tuple-element.98), channel_id=1, source_target_pairs={{8,24},{12,28},{9,25},{13,29},{10,26},{14,30},{11,27},{15,31}} | collective-permute-start | bytes 393224 | tf_op jit(solution)/shard_map/ppermute | solution.py:301
  24.9 6.5 %collective-permute-start.4 = (f32[2,128,128]{2,1,0:T(8,128)S(1)}, f32[2,128,128]{2,1,0:T(8,128)S(1)}, u32[]{:S(2)}, u32[]{:S(2)}) collective-permute-start(f32[2,128,128]{2,1,0:T(8,128)S(1)} %get-tuple-element.99), channel_id=1, source_target_pairs={{8,16},{12,20},{9,17},{13,21},{10,18},{14,22},{11,19},{15,23}} | collective-permute-start | bytes 393224 | tf_op jit(solution)/shard_map/ppermute | solution.py:301
  25.5 19.8 %collective-permute-start.2 = (f32[4,128,128]{2,1,0:T(8,128)S(1)}, f32[4,128,128]{2,1,0:T(8,128)S(1)}, u32[]{:S(2)}, u32[]{:S(2)}) collective-permute-start(f32[4,128,128]{2,1,0:T(8,128)S(1)} %states.2), channel_id=1, source_target_pairs={{0,4},{8,12},{16,20},{24,28},{1,5},{9,13},{17,21},{25,29},{2,6},{1... | collective-permute-start | bytes 786440 | tf_op jit(solution)/shard_map/ppermute | solution.py:301
  29.0 16.4 %collective-permute-start.3 = (f32[4,128,128]{2,1,0:T(8,128)S(1)}, f32[4,128,128]{2,1,0:T(8,128)S(1)}, u32[]{:S(2)}, u32[]{:S(2)}) collective-permute-start(f32[4,128,128]{2,1,0:T(8,128)S(1)} %collective-permute-done.1.refs_2_), channel_id=1, source_target_pairs={{8,12},{12,8},{24,28},{28,24},{9,13},{13,9},{25,29},{29,25},{10,14... | collective-permute-start | bytes 786440 | tf_op jit(solution)/shard_map/ppermute | solution.py:301
  31.3 14.1 %copy-start.5 = (bf16[1024,1024]{1,0:T(8,128)(2,1)S(1)}, bf16[1024,1024]{1,0:T(8,128)(2,1)}, u32[]{:S(2)}) copy-start(bf16[1024,1024]{1,0:T(8,128)(2,1)} %cot_ref.3) | copy-start | bytes 6291460
  31.4 14.1 %copy-start.6 = (f32[4,8,1024]{2,1,0:T(8,128)S(1)}, f32[4,8,1024]{2,1,0:T(8,128)}, u32[]{:S(2)}) copy-start(f32[4,8,1024]{2,1,0:T(8,128)} %coef_ref.7) | copy-start | bytes 393220
  31.4 14.0 %copy-start.7 = (f32[1024]{0:T(1024)S(1)}, f32[1024]{0:T(1024)}, u32[]{:S(2)}) copy-start(f32[1024]{0:T(1024)} %param.10) | copy-start | bytes 12292
  31.4 14.0 %collective-permute-start.8 = (f32[2,128,128]{2,1,0:T(8,128)S(1)}, f32[2,128,128]{2,1,0:T(8,128)S(1)}, u32[]{:S(2)}, u32[]{:S(2)}) collective-permute-start(f32[2,128,128]{2,1,0:T(8,128)S(1)} %add.42.refs_4_), channel_id=1, source_target_pairs={{16,28},{20,24},{24,20},{28,16},{17,29},{21,25},{25,21},{29,17},{1... | collective-permute-start | bytes 393224 | tf_op jit(solution)/shard_map/ppermute | solution.py:301
  36.3 9.0 %collective-permute-start.7 = (f32[2,128,128]{2,1,0:T(8,128)S(1)}, f32[2,128,128]{2,1,0:T(8,128)S(1)}, u32[]{:S(2)}, u32[]{:S(2)}) collective-permute-start(f32[2,128,128]{2,1,0:T(8,128)S(1)} %add.42.refs_4_), channel_id=1, source_target_pairs={{16,24},{20,28},{24,16},{28,20},{17,25},{21,29},{25,17},{29,21},{1... | collective-permute-start | bytes 393224 | tf_op jit(solution)/shard_map/ppermute | solution.py:301
  38.4 7.0 %collective-permute-start.6 = (f32[2,128,128]{2,1,0:T(8,128)S(1)}, f32[2,128,128]{2,1,0:T(8,128)S(1)}, u32[]{:S(2)}, u32[]{:S(2)}) collective-permute-start(f32[2,128,128]{2,1,0:T(8,128)S(1)} %add.42.refs_4_), channel_id=1, source_target_pairs={{16,20},{20,16},{24,28},{28,24},{17,21},{21,17},{25,29},{29,25},{1... | collective-permute-start | bytes 393224 | tf_op jit(solution)/shard_map/ppermute | solution.py:301
  54.4 1.2 collective-permute-start.9
  55.6 3.7 %collective-permute-start.10 = (f32[2,1024]{1,0:T(2,128)S(1)}, f32[2,1024]{1,0:T(2,128)S(1)}, u32[]{:S(2)}, u32[]{:S(2)}) collective-permute-start(f32[2,1024]{1,0:T(2,128)S(1)} %add.43), channel_id=1, source_target_pairs={{0,2},{1,3},{2,0},{3,1},{4,6},{5,7},{6,4},{7,5},{8,10},{9,11},{10,... | collective-permute-start | bytes 24584 | tf_op jit(solution)/shard_map/ppermute | solution.py:458
  59.2 13.6 %copy-start.3 = (bf16[1024,1024]{1,0:T(8,128)(2,1)S(1)}, bf16[1024,1024]{1,0:T(8,128)(2,1)}, u32[]{:S(2)}) copy-start(bf16[1024,1024]{1,0:T(8,128)(2,1)} %value_ref.17) | copy-start | bytes 6291460
  65.7 14.9 %collective-permute-start.14 = (f32[4,128,128]{2,1,0:T(8,128)S(1)}, f32[4,128,128]{2,1,0:T(8,128)S(1)}, u32[]{:S(2)}, u32[]{:S(2)}) collective-permute-start(f32[4,128,128]{2,1,0:T(8,128)S(1)} %get-tuple-element.65), channel_id=1, source_target_pairs={{8,12},{12,8},{24,28},{28,24},{9,13},{13,9},{25,29},{29,25},{10,14... | collective-permute-start | bytes 786440 | tf_op jit(solution)/shard_map/ppermute | solution.py:301
  69.2 11.4 %collective-permute-start.11 = (f32[264,128]{1,0:T(8,128)S(1)}, f32[264,128]{1,0:T(8,128)S(1)}, u32[]{:S(2)}, u32[]{:S(2)}) collective-permute-start(f32[264,128]{1,0:T(8,128)S(1)} %get-tuple-element.62), channel_id=1, source_target_pairs={{0,4},{4,0},{8,12},{12,8},{16,20},{20,16},{24,28},{28,24},{1,5},{5... | collective-permute-start | bytes 405512 | tf_op jit(solution)/shard_map/ppermute | solution.py:301
  69.7 10.9 %collective-permute-start.12 = (f32[264,128]{1,0:T(8,128)S(1)}, f32[264,128]{1,0:T(8,128)S(1)}, u32[]{:S(2)}, u32[]{:S(2)}) collective-permute-start(f32[264,128]{1,0:T(8,128)S(1)} %get-tuple-element.63), channel_id=1, source_target_pairs={{0,8},{4,12},{8,0},{12,4},{16,24},{20,28},{24,16},{28,20},{1,9},{5... | collective-permute-start | bytes 405512 | tf_op jit(solution)/shard_map/ppermute | solution.py:301
  69.9 10.7 %collective-permute-start.13 = (f32[264,128]{1,0:T(8,128)S(1)}, f32[264,128]{1,0:T(8,128)S(1)}, u32[]{:S(2)}, u32[]{:S(2)}) collective-permute-start(f32[264,128]{1,0:T(8,128)S(1)} %get-tuple-element.64), channel_id=1, source_target_pairs={{0,12},{4,8},{8,4},{12,0},{16,28},{20,24},{24,20},{28,16},{1,13},{... | collective-permute-start | bytes 405512 | tf_op jit(solution)/shard_map/ppermute | solution.py:301
  80.7 10.1 %collective-permute-start.16 = (f32[264,128]{1,0:T(8,128)S(1)}, f32[264,128]{1,0:T(8,128)S(1)}, u32[]{:S(2)}, u32[]{:S(2)}) collective-permute-start(f32[264,128]{1,0:T(8,128)S(1)} %add_add_fusion.sum_ref), channel_id=1, source_target_pairs={{8,24},{12,28},{24,8},{28,12},{9,25},{13,29},{25,9},{29,13},{10,26... | collective-permute-start | bytes 405512 | tf_op jit(solution)/shard_map/ppermute | solution.py:301
  82.6 8.2 %collective-permute-start.15 = (f32[264,128]{1,0:T(8,128)S(1)}, f32[264,128]{1,0:T(8,128)S(1)}, u32[]{:S(2)}, u32[]{:S(2)}) collective-permute-start(f32[264,128]{1,0:T(8,128)S(1)} %add_add_fusion.sum_ref), channel_id=1, source_target_pairs={{8,16},{12,20},{16,8},{20,12},{9,17},{13,21},{17,9},{21,13},{10,18... | collective-permute-start | bytes 405512 | tf_op jit(solution)/shard_map/ppermute | solution.py:301
  91.4 15.2 %collective-permute-start.17 = (f32[520,128]{1,0:T(8,128)S(1)}, f32[520,128]{1,0:T(8,128)S(1)}, u32[]{:S(2)}, u32[]{:S(2)}) collective-permute-start(f32[520,128]{1,0:T(8,128)S(1)} %lower.1.lowered_ref), channel_id=1, source_target_pairs={{8,0},{12,4},{24,16},{28,20},{9,1},{13,5},{25,17},{29,21},{10,2},{... | collective-permute-start | bytes 798728 | tf_op jit(solution)/shard_map/ppermute | solution.py:301
  98.0 19.6 %collective-permute-start.18 = (f32[4,128,128]{2,1,0:T(8,128)S(1)}, f32[4,128,128]{2,1,0:T(8,128)S(1)}, u32[]{:S(2)}, u32[]{:S(2)}) collective-permute-start(f32[4,128,128]{2,1,0:T(8,128)S(1)} %get-tuple-element.92), channel_id=1, source_target_pairs={{4,0},{12,8},{20,16},{28,24},{5,1},{13,9},{21,17},{29,25},{6,2},{1... | collective-permute-start | bytes 786440 | tf_op jit(solution)/shard_map/ppermute | solution.py:301
  107.7 9.9 %collective-permute-start.19 = (f32[4,128,128]{2,1,0:T(8,128)S(1)}, f32[4,128,128]{2,1,0:T(8,128)S(1)}, u32[]{:S(2)}, u32[]{:S(2)}) collective-permute-start(f32[4,128,128]{2,1,0:T(8,128)S(1)} %get-tuple-element.93), channel_id=1, source_target_pairs={{0,4},{4,0},{8,12},{12,8},{16,20},{20,16},{24,28},{28,24},{1,5},{5... | collective-permute-start | bytes 786440 | tf_op jit(solution)/shard_map/ppermute | solution.py:301
